TPU v7x, 128 devices: a whole 4x4x4 slice. The times are simulated.
128 devices in a mesh: tm: 4 (over y_lo, core), space: 32 (over x, y_hi, z).
Axes of the slice: x: 4, y: 4 (y_hi: 2, y_lo: 2; y = y_hi * 2 + y_lo), z: 4, core: 2. Of those that a mesh axis runs over, the one named last changes fastest.
Arguments:
- queries: bfloat16 [4, 32, 384, 1536], P('tm', 'space'), may hold values from -7 to 7
- keys: bfloat16 [4, 32, 384, 1536], P('tm', 'space'), may hold values from -7 to 7
- values: bfloat16 [4, 32, 384, 1536], P('tm', 'space'), may hold values from -2 to 2
- outputs: bfloat16 [4, 32, 384, 1536], P('tm', 'space'), may hold values from -2 to 2
- out_grads: bfloat16 [4, 32, 384, 1536], P('tm', 'space'), may hold values from -6 to 6
- log_sums: float32 [4, 32, 12, 384], P('tm', 'space'), may hold values from 8 to 9.5
- window_mask: int32 [4, 32, 9], P('tm', 'space'), may hold values 0 or 1
Outputs:
- query_grads: bfloat16 [4, 32, 384, 1536], P('tm', 'space')
- key_grads: bfloat16 [4, 32, 384, 1536], P('tm', 'space')
- value_grads: bfloat16 [4, 32, 384, 1536], P('tm', 'space')
All inputs are finite; a program needn't handle non-finite values. No bound on the sum of `window_mask` on one device may be relied on, other than what follows from the above.
Results may differ from a plain program's by a relative error of at most 0.0065.
Values may be sent and summed in bfloat16 or wider, within the bound.
A program may use at most 192 MiB of HBM per device.

v0:
```python
import jax
import jax.numpy as jnp
from jax import lax
from jax.sharding import PartitionSpec as P


def with_halo(shard, sides, width):
    for axis, dim in sides:
        peers, length = (lax.axis_size(axis), shard.shape[dim])
        up = [(i, (i + 1) % peers) for i in range(peers - 1)]
        down = [(j, i) for i, j in up]
        last = lax.slice_in_dim(shard, length - width, length, axis=dim)
        initial = lax.slice_in_dim(shard, 0, width, axis=dim)
        before = lax.ppermute(last, axis, up)
        after = lax.ppermute(initial, axis, down)
        shard = jnp.concatenate([before, shard, after], axis=dim)
    return shard


def from_behind(value, axis, steps):
    count = lax.axis_size(axis)
    initial, last = (max(0, -steps), min(count, count - steps))
    return lax.ppermute(value, axis, [(source, source + steps) for source in range(initial, last)])


def round_keep(value):
    return lax.optimization_barrier(value.astype(jnp.bfloat16)).astype(jnp.float32)


def pair_terms(query_rows, grad_rows, sum_rows, delta_rows, flags, key_rows, value_rows):
    num_tiles, tile_len, full_width = query_rows.shape
    head_count = sum_rows.shape[1]
    head_width = full_width // head_count
    factor = head_width ** (-0.5)
    shape_four = (num_tiles, tile_len, head_count, head_width)
    query_heads = query_rows.reshape(shape_four)
    grad_heads = grad_rows.reshape(shape_four)
    key_heads = key_rows.reshape(shape_four)
    value_heads = value_rows.reshape(shape_four)
    scores = (
        jnp.einsum("nqhd,nkhd->nhqk", query_heads, key_heads, preferred_element_type=jnp.float32)
        * factor
    )
    weights = jnp.exp(scores - sum_rows[..., None]) * flags[:, None, None, None]
    weights_low = weights.astype(jnp.bfloat16)
    grad_prob = jnp.einsum(
        "nqhd,nkhd->nhqk", grad_heads, value_heads, preferred_element_type=jnp.float32
    )
    grad_score = (weights * (grad_prob - delta_rows[..., None])).astype(jnp.bfloat16)
    query_term = (
        jnp.einsum("nhqk,nkhd->nqhd", grad_score, key_heads, preferred_element_type=jnp.float32)
        * factor
    )
    key_term = (
        jnp.einsum("nhqk,nqhd->nkhd", grad_score, query_heads, preferred_element_type=jnp.float32)
        * factor
    )
    value_term = jnp.einsum(
        "nhqk,nqhd->nkhd", weights_low, grad_heads, preferred_element_type=jnp.float32
    )
    flat = (num_tiles, tile_len, full_width)
    return (query_term.reshape(flat), key_term.reshape(flat), value_term.reshape(flat))


def spread(minus, centre, plus, axis_dim):
    count = centre.shape[axis_dim]
    zero_shape = list(centre.shape)
    zero_shape[axis_dim] = 1
    zero_row = jnp.zeros(tuple(zero_shape), centre.dtype)
    lower = jnp.concatenate((lax.slice_in_dim(minus, 1, count, 1, axis_dim), zero_row), axis_dim)
    upper = jnp.concatenate((zero_row, lax.slice_in_dim(plus, 0, count - 1, 1, axis_dim)), axis_dim)
    interior = centre + lower + upper
    rim_before = lax.index_in_dim(minus, 0, axis_dim, False)
    rim_after = lax.index_in_dim(plus, count - 1, axis_dim, False)
    return (interior, rim_before, rim_after)


def per_device(queries, keys, values, outputs, out_grads, log_sums, window_mask):
    time_tiles, row_tiles, tile_len, full_width = queries.shape
    head_count = log_sums.shape[2]
    head_width = full_width // head_count
    num_tiles = time_tiles * row_tiles
    all_times = time_tiles * lax.axis_size("tm")
    all_rows = row_tiles * lax.axis_size("space")
    first_time = lax.axis_index("tm") * time_tiles
    first_row = lax.axis_index("space") * row_tiles
    products = out_grads.astype(jnp.float32) * outputs.astype(jnp.float32)
    deltas = (
        products.reshape(time_tiles, row_tiles, tile_len, head_count, head_width)
        .sum(-1)
        .transpose(0, 1, 3, 2)
    )
    flat = (num_tiles, tile_len, full_width)
    query_flat = queries.reshape(flat)
    grad_flat = out_grads.reshape(flat)
    sums_flat = log_sums.reshape(num_tiles, head_count, tile_len)
    deltas_flat = deltas.reshape(num_tiles, head_count, tile_len)
    pair_kv = with_halo(jnp.stack((keys, values)), (("tm", 1), ("space", 2)), 1)
    times_here = first_time + jnp.arange(time_tiles, dtype=jnp.int32)
    rows_here = first_row + jnp.arange(row_tiles, dtype=jnp.int32)
    query_total = jnp.zeros(flat, jnp.float32)
    interiors = []
    befores = []
    afters = []
    for time_off in (-1, 0, 1):
        pieces = []
        for row_off in (-1, 0, 1):
            slab = pair_kv[
                :, 1 + time_off : 1 + time_off + time_tiles, 1 + row_off : 1 + row_off + row_tiles
            ]
            slab = slab.reshape((2,) + flat)
            time_inside = jnp.logical_and(
                times_here + time_off >= 0, times_here + time_off < all_times
            )
            row_inside = jnp.logical_and(rows_here + row_off >= 0, rows_here + row_off < all_rows)
            inside = jnp.logical_and(time_inside[:, None], row_inside[None, :])
            slot_index = (time_off + 1) * 3 + row_off + 1
            if slot_index == 4:
                picked = inside
            else:
                picked = jnp.logical_and(inside, window_mask[:, :, slot_index] > 0)
            query_term, key_term, value_term = pair_terms(
                query_flat,
                grad_flat,
                sums_flat,
                deltas_flat,
                picked.astype(jnp.float32).reshape(num_tiles),
                slab[0],
                slab[1],
            )
            query_total = query_total + query_term
            pieces.append(
                round_keep(jnp.stack((key_term, value_term))).reshape(
                    2, time_tiles, row_tiles, tile_len, full_width
                )
            )
        interior, rim_before, rim_after = spread(pieces[0], pieces[1], pieces[2], 2)
        interiors.append(interior)
        befores.append(rim_before)
        afters.append(rim_after)
    rim_before = jnp.stack(befores, 1).astype(jnp.bfloat16)
    rim_after = jnp.stack(afters, 1).astype(jnp.bfloat16)
    from_before = from_behind(rim_after, "space", 1)
    from_after = from_behind(rim_before, "space", -1)
    own_rows = jnp.stack(interiors, 1)
    own_rows = own_rows.at[:, :, :, 0].add(from_before.astype(jnp.float32))
    own_rows = own_rows.at[:, :, :, row_tiles - 1].add(from_after.astype(jnp.float32))
    grouped = own_rows.astype(jnp.bfloat16)
    own_times, edge_before, edge_after = spread(
        grouped[:, 0].astype(jnp.float32),
        grouped[:, 1].astype(jnp.float32),
        grouped[:, 2].astype(jnp.float32),
        1,
    )
    from_past = from_behind(edge_after.astype(jnp.bfloat16), "tm", 1)
    from_future = from_behind(edge_before.astype(jnp.bfloat16), "tm", -1)
    own_times = own_times.at[:, 0].add(from_past.astype(jnp.float32))
    own_times = own_times.at[:, time_tiles - 1].add(from_future.astype(jnp.float32))
    key_grads = own_times[0].astype(jnp.bfloat16)
    value_grads = own_times[1].astype(jnp.bfloat16)
    query_grads = query_total.astype(jnp.bfloat16).reshape(
        time_tiles, row_tiles, tile_len, full_width
    )
    return (query_grads, key_grads, value_grads)


def solution(mesh):
    return jax.shard_map(
        per_device,
        mesh=mesh,
        in_specs=(
            P("tm", "space", None, None),
            P("tm", "space", None, None),
            P("tm", "space", None, None),
            P("tm", "space", None, None),
            P("tm", "space", None, None),
            P("tm", "space", None, None),
            P("tm", "space", None),
        ),
        out_specs=(
            P("tm", "space", None, None),
            P("tm", "space", None, None),
            P("tm", "space", None, None),
        ),
        check_vma=False,
    )
```

profile of v0, /device:TPU:5, one launch (start us, length us, event | category | flops | bytes accessed | tf_op | source)
XLA Modules:
  0.0 577.4 jit_solution(10623707769678440699)
XLA Ops:
  9.3 176.3 %collective-permute-done.1 = bf16[2,1,1,384,1536]{3,4,2,1,0:T(8,128)(2,1)S(1)} collective-permute-done((bf16[2,1,1,384,1536]{3,4,2,1,0:T(8,128)(2,1)S(1)}, bf16[2,1,1,384,1536]{3,4,2,1,0:T(8,128)(2,1)S(1)}, u32[]{:S(2)}, u32[]{:S(2)}) %collective-permute-start.1) | collective-permute-done | bytes 2359328 | tf_op jit(solution)/shard_map/ppermute | solution.py:15
  186.8 3.7 pad_maximum_fusion
  216.8 5.5 multiply_convert_fusion.8
  232.9 3.8 collective-permute-start.2
  236.7 34.5 %collective-permute-done.3 = bf16[2,3,1,384,1536]{3,4,2,1,0:T(8,128)(2,1)} collective-permute-done((bf16[2,3,1,384,1536]{3,4,2,1,0:T(8,128)(2,1)}, bf16[2,3,1,384,1536]{3,4,2,1,0:T(8,128)(2,1)}, u32[]{:S(2)}, u32[]{:S(2)}) %collective-permute-start.3) | collective-permute-done | bytes 7077920 | tf_op jit(solution)/shard_map/ppermute | solution.py:15
  271.2 5.5 fusion.98
  283.7 5.3 multiply_convert_fusion
  303.9 5.3 multiply_convert_fusion.3
  324.2 5.1 multiply_convert_fusion.5
  336.8 3.4 pad_maximum_fusion.1
  342.1 38.4 %collective-permute-done.2 = bf16[2,3,1,384,1536]{3,4,2,1,0:T(8,128)(2,1)} collective-permute-done((bf16[2,3,1,384,1536]{3,4,2,1,0:T(8,128)(2,1)}, bf16[2,3,1,384,1536]{3,4,2,1,0:T(8,128)(2,1)}, u32[]{:S(2)}, u32[]{:S(2)}) %collective-permute-start.2) | collective-permute-done | bytes 7077920 | tf_op jit(solution)/shard_map/ppermute | solution.py:14
  380.5 5.2 fusion.99
  389.6 4.0 multiply_convert_fusion.2
  396.1 4.2 multiply_convert_fusion.9
  409.8 4.0 multiply_convert_fusion.4
  416.2 4.3 multiply_convert_fusion.10
  456.3 5.3 multiply_convert_fusion.6
  478.0 5.3 multiply_convert_fusion.1
  496.6 30.0 %collective-permute-done.5 = bf16[2,3,1,384,1536]{4,3,0,1,2:T(8,128)(2,1)} collective-permute-done((bf16[2,3,1,384,1536]{4,3,0,1,2:T(8,128)(2,1)}, bf16[2,3,1,384,1536]{4,3,0,1,2:T(8,128)(2,1)}, u32[]{:S(2)}, u32[]{:S(2)}) %collective-permute-start.5) | collective-permute-done | bytes 7077920 | tf_op jit(solution)/shard_map/ppermute | solution.py:23
  526.7 6.7 %fusion = bf16[2,3,1,1,384,1536]{5,4,0,3,2,1:T(8,128)(2,1)S(1)} fusion(bf16[2,1,1,1,384,1536]{5,4,0,3,2,1:T(8,128)(2,1)S(1)} %bitcast.378, bf16[2,1,1,1,384,1536]{5,4,0,3,2,1:T(8,128)(2,1)S(1)} %bitcast.376, bf16[2,1,1,1,384,1536]{5,4,0,3,2,1:T(8,128)(2,1)S(1)} %bitcast.377, bf16[2,3,1,384,1536]{4,3,0,1,2:T(8,128)(2,1)} %collective-permute-done.5, ...), kind=kLoop, calls=%fused_computation.1 | loop fusion | flops 28311552 | bytes 28311552 | tf_op jit(solution)/shard_map/convert_element_type | solution.py:148
  540.8 4.1 collective-permute-start.7
  556.6 10.3 %collective-permute-done.6 = bf16[2,1,384,1536]{3,2,0,1:T(8,128)(2,1)} collective-permute-done((bf16[2,1,384,1536]{3,2,0,1:T(8,128)(2,1)}, bf16[2,1,384,1536]{3,2,0,1:T(8,128)(2,1)}, u32[]{:S(2)}, u32[]{:S(2)}) %collective-permute-start.6) | collective-permute-done | bytes 2359328 | tf_op jit(solution)/shard_map/ppermute | solution.py:23
  566.9 4.7 collective-permute-done.7
  571.6 4.0 fusion.10
  (224 shorter events, 191.6 us)
Async XLA Ops:
  3.2 183.6 %copy-start.9 = (bf16[1,1,384,1536]{2,3,1,0:T(8,128)(2,1)}, bf16[1,1,384,1536]{2,3,1,0:T(8,128)(2,1)S(1)}, u32[]{:S(2)}) copy-start(bf16[1,1,384,1536]{2,3,1,0:T(8,128)(2,1)S(1)} %copy.78) | copy-start | bytes 3538948
  3.5 188.9 %copy-start.67 = (s32[1,1,9]{2,1,0:T(1,128)S(1)}, s32[1,1,9]{2,1,0:T(1,128)}, u32[]{:S(2)}) copy-start(s32[1,1,9]{2,1,0:T(1,128)} %param.21) | copy-start | bytes 112
  3.5 194.9 %copy-start.68 = (f32[1,1,12,384]{3,1,2,0:T(1,128)S(1)}, f32[1,1,12,384]{3,1,2,0:T(1,128)}, u32[]{:S(2)}) copy-start(f32[1,1,12,384]{3,1,2,0:T(1,128)} %param.20) | copy-start | bytes 55300
  3.5 182.1 %collective-permute-start.1 = (bf16[2,1,1,384,1536]{3,4,2,1,0:T(8,128)(2,1)S(1)}, bf16[2,1,1,384,1536]{3,4,2,1,0:T(8,128)(2,1)S(1)}, u32[]{:S(2)}, u32[]{:S(2)}) collective-permute-start(bf16[2,1,1,384,1536]{3,4,2,1,0:T(8,128)(2,1)S(1)} %pad_maximum_fusion.3), channel_id=1, source_target_pairs={{32,0},{64,32},{96,64},{33,1},{65,33},{97,65},{34,2},{66,34},{98,6... | collective-permute-start | bytes 7077896 | tf_op jit(solution)/shard_map/ppermute | solution.py:15
  6.2 180.6 %collective-permute-start = (bf16[2,1,1,384,1536]{3,4,2,1,0:T(8,128)(2,1)S(1)}, bf16[2,1,1,384,1536]{3,4,2,1,0:T(8,128)(2,1)S(1)}, u32[]{:S(2)}, u32[]{:S(2)}) collective-permute-start(bf16[2,1,1,384,1536]{3,4,2,1,0:T(8,128)(2,1)S(1)} %pad_maximum_fusion.3), channel_id=1, source_target_pairs={{0,32},{32,64},{64,96},{1,33},{33,65},{65,97},{2,34},{34,66},{66,9... | collective-permute-start | bytes 7077896 | tf_op jit(solution)/shard_map/ppermute | solution.py:14
  185.6 4.9 copy-start.41
  186.8 3.7 copy-start.43
  190.5 80.7 %collective-permute-start.3 = (bf16[2,3,1,384,1536]{3,4,2,1,0:T(8,128)(2,1)}, bf16[2,3,1,384,1536]{3,4,2,1,0:T(8,128)(2,1)}, u32[]{:S(2)}, u32[]{:S(2)}) collective-permute-start(bf16[2,3,1,384,1536]{3,4,2,1,0:T(8,128)(2,1)} %pad_maximum_fusion), channel_id=1, source_target_pairs={{1,0},{2,1},{3,2},{4,3},{5,4},{6,5},{7,6},{8,7},{9,8},{10,9},{11,1... | collective-permute-start | bytes 21233672 | tf_op jit(solution)/shard_map/ppermute | solution.py:15
  226.9 3.4 copy-start.1
  232.9 147.6 %collective-permute-start.2 = (bf16[2,3,1,384,1536]{3,4,2,1,0:T(8,128)(2,1)}, bf16[2,3,1,384,1536]{3,4,2,1,0:T(8,128)(2,1)}, u32[]{:S(2)}, u32[]{:S(2)}) collective-permute-start(bf16[2,3,1,384,1536]{3,4,2,1,0:T(8,128)(2,1)} %pad_maximum_fusion), channel_id=1, source_target_pairs={{0,1},{1,2},{2,3},{3,4},{4,5},{5,6},{6,7},{7,8},{8,9},{9,10},{10,1... | collective-permute-start | bytes 21233672 | tf_op jit(solution)/shard_map/ppermute | solution.py:14
  276.8 40.5 %copy-start.24 = (bf16[1,1,1,384,1536]{3,4,2,1,0:T(8,128)(2,1)}, bf16[1,1,1,384,1536]{3,4,2,1,0:T(8,128)(2,1)S(1)}, u32[]{:S(2)}) copy-start(bf16[1,1,1,384,1536]{3,4,2,1,0:T(8,128)(2,1)S(1)} %get-tuple-element.64) | copy-start | bytes 3538948
  340.2 156.4 %collective-permute-start.4 = (bf16[2,3,1,384,1536]{4,3,0,1,2:T(8,128)(2,1)}, bf16[2,3,1,384,1536]{4,3,0,1,2:T(8,128)(2,1)}, u32[]{:S(2)}, u32[]{:S(2)}) collective-permute-start(bf16[2,3,1,384,1536]{4,3,0,1,2:T(8,128)(2,1)} %pad_maximum_fusion.1), channel_id=1, source_target_pairs={{0,1},{1,2},{2,3},{3,4},{4,5},{5,6},{6,7},{7,8},{8,9},{9,10},{10,1... | collective-permute-start | bytes 21233672 | tf_op jit(solution)/shard_map/ppermute | solution.py:23
  442.8 5.4 copy-start.44
  446.2 80.5 %collective-permute-start.5 = (bf16[2,3,1,384,1536]{4,3,0,1,2:T(8,128)(2,1)}, bf16[2,3,1,384,1536]{4,3,0,1,2:T(8,128)(2,1)}, u32[]{:S(2)}, u32[]{:S(2)}) collective-permute-start(bf16[2,3,1,384,1536]{4,3,0,1,2:T(8,128)(2,1)} %pad_maximum_fusion.2), channel_id=1, source_target_pairs={{1,0},{2,1},{3,2},{4,3},{5,4},{6,5},{7,6},{8,7},{9,8},{10,9},{11,1... | collective-permute-start | bytes 21233672 | tf_op jit(solution)/shard_map/ppermute | solution.py:23
  466.4 3.4 copy-start.42
  495.7 31.0 %copy-start.39 = (bf16[2,1,384,1536]{3,2,0,1:T(8,128)(2,1)S(1)}, bf16[2,1,384,1536]{3,2,0,1:T(8,128)(2,1)}, u32[]{:S(2)}) copy-start(bf16[2,1,384,1536]{3,2,0,1:T(8,128)(2,1)} %pad_maximum_fusion.5) | copy-start | bytes 7077892
  495.7 31.0 %copy-start.40 = (bf16[2,1,384,1536]{3,2,0,1:T(8,128)(2,1)S(1)}, bf16[2,1,384,1536]{3,2,0,1:T(8,128)(2,1)}, u32[]{:S(2)}) copy-start(bf16[2,1,384,1536]{3,2,0,1:T(8,128)(2,1)} %pad_maximum_fusion.4) | copy-start | bytes 7077892
  533.4 5.5 copy-start.2
  533.4 11.5 %copy-start.11 = (bf16[12,384,384]{2,1,0:T(8,128)(2,1)S(1)}, bf16[12,384,384]{2,1,0:T(8,128)(2,1)}, u32[]{:S(2)}) copy-start(bf16[12,384,384]{2,1,0:T(8,128)(2,1)} %copy-done.10) | copy-start | bytes 10616836
  533.4 11.5 %copy-start.27 = (bf16[1,1,1,384,1536]{3,4,2,1,0:T(8,128)(2,1)S(1)}, bf16[1,1,1,384,1536]{3,4,2,1,0:T(8,128)(2,1)}, u32[]{:S(2)}) copy-start(bf16[1,1,1,384,1536]{3,4,2,1,0:T(8,128)(2,1)} %get-tuple-element.62) | copy-start | bytes 3538948
  538.9 28.0 %collective-permute-start.6 = (bf16[2,1,384,1536]{3,2,0,1:T(8,128)(2,1)}, bf16[2,1,384,1536]{3,2,0,1:T(8,128)(2,1)}, u32[]{:S(2)}, u32[]{:S(2)}) collective-permute-start(bf16[2,1,384,1536]{3,2,0,1:T(8,128)(2,1)} %get-tuple-element.57), channel_id=1, source_target_pairs={{0,32},{32,64},{64,96},{1,33},{33,65},{65,97},{2,34},{34,66},{66,9... | collective-permute-start | bytes 7077896 | tf_op jit(solution)/shard_map/ppermute | solution.py:23
  540.8 5.1 copy-start.13
  540.8 5.1 copy-start.25
  540.8 30.7 %collective-permute-start.7 = (bf16[2,1,384,1536]{3,2,0,1:T(8,128)(2,1)}, bf16[2,1,384,1536]{3,2,0,1:T(8,128)(2,1)}, u32[]{:S(2)}, u32[]{:S(2)}) collective-permute-start(bf16[2,1,384,1536]{3,2,0,1:T(8,128)(2,1)} %get-tuple-element.58), channel_id=1, source_target_pairs={{32,0},{64,32},{96,64},{33,1},{65,33},{97,65},{34,2},{66,34},{98,6... | collective-permute-start | bytes 7077896 | tf_op jit(solution)/shard_map/ppermute | solution.py:23
  (53 other events, 117.7 us)
where the time goes:
time: 585 us; the launch traced here: 577 us
  waiting for transfers between devices  295 us (50%)
  matrix products  115 us (20%)
  local copies, waits for them, and re-layouts  86.4 us (15%)
  other arithmetic  52.1 us (9%)
  starting transfers between devices  21.4 us (4%)
  between operations  6.9 us (1%)
    ppermute x2, waiting for transfers between devices, with_halo(): after = lax.ppermute(initial, axis, down)  211 us
    ppermute x4, waiting for transfers between devices, from_behind(): lax.ppermute(value, axis, [(source, source + steps) for source in range(i...  45 us
    another operation x18, local copies, waits for them, and re-layouts, per_device(): jnp.stack((key_term, value_term))  44.4 us
    dot_general x9, matrix products, pair_terms(): jnp.einsum('nqhd,nkhd->nhqk', grad_heads, value_heads, preferred_element_...  42 us
    ppermute x2, waiting for transfers between devices, with_halo(): before = lax.ppermute(last, axis, up)  39.5 us
    dot_general x9, matrix products, pair_terms(): jnp.einsum('nhqk,nqhd->nkhd', weights_low, grad_heads, preferred_element_...  28 us
    another operation x9, other arithmetic, per_device(): jnp.stack((key_term, value_term))  25.2 us
    dot_general x9, matrix products, pair_terms(): jnp.einsum('nhqk,nqhd->nkhd', grad_score, query_heads, preferred_element_...  24.1 us
  transfers between devices with their start and end apart: 8, of which 7 were waited for; matrix products, arithmetic and copies ran while one was open for 38% of the time, Pallas kernels for 0%

commit v1 on v0

v1 whole, which is shorter than its diff:
```python
import functools
import math

import jax
import jax.numpy as jnp
from jax import lax
from jax.experimental import pallas as pl
from jax.experimental.pallas import tpu as pltpu
from jax.sharding import PartitionSpec as P

F32 = jnp.float32
LOW = jnp.bfloat16
MESH = pl.DeviceIdType.MESH
GROUP = 1
EARLY = 2
LOG2E = math.log2(math.e)
NT = (((1,), (1,)), ((), ()))
NN = (((1,), (0,)), ((), ()))
TN = (((0,), (0,)), ((), ()))
OWN, UP, DOWN = 0, 1, 2
CHIP, LINK = 1, 2
DELTA_ROW, PEN_ROW, AUX_ROWS = 16, 32, 48


def dot(a, b, dims):
    return lax.dot_general(a, b, dims, preferred_element_type=F32)


def kernel(
    q_in, k_in, v_in, o_in, g_in, lse_ref, mask_ref,
    dq_out, dk_out, dv_out,
    qs, gs, ks, vs, outs, aux, dq_acc, dq_own, dk_own, dv_own,
    dq_send, dk_send, dv_send, dq_recv, dk_recv, dv_recv,
    in_sem, q_ss, q_rs, kv_ss, kv_rs, aux_ss, aux_rs, dq_ss, dq_rs, dkv_ss, dkv_rs,
):
    tile, full = q_in.shape
    heads = lse_ref.shape[0]
    width = full // heads
    wide = GROUP * width
    chunks = heads // GROUP
    scale = width**-0.5
    frame, row = lax.axis_index("tm"), lax.axis_index("space")
    frames, rows = lax.axis_size("tm"), lax.axis_size("space")
    odd = lax.rem(frame, 2)
    step = 1 - 2 * odd
    has_up, has_down = row < rows - 1, row > 0
    other = frame - step
    has_link = jnp.logical_and(other >= 0, other < frames)
    to_up, to_down = (frame, row + 1), (frame, row - 1)
    to_chip, to_link = (frame + step, row), (other, row)
    row_sides = ((has_up, to_up, UP, DOWN), (has_down, to_down, DOWN, UP))

    def cols(c):
        return pl.ds(pl.multiple_of(c * wide, wide), wide)

    def head_cols(h):
        return pl.ds(pl.multiple_of(h * width, width), width)

    local = [
        pltpu.make_async_copy(src, dst, in_sem.at[i])
        for i, (src, dst) in enumerate(
            ((o_in, outs), (g_in, gs.at[OWN]), (q_in, qs.at[OWN]), (k_in, ks.at[0]), (v_in, vs.at[0]))
        )
    ]
    for copy in local:
        copy.start()

    barrier = pltpu.get_barrier_semaphore()
    pl.semaphore_signal(barrier, inc=1, device_id=to_chip, device_id_type=MESH)
    for there, dst in ((has_up, to_up), (has_down, to_down), (has_link, to_link)):
        @pl.when(there)
        def _():
            pl.semaphore_signal(barrier, inc=1, device_id=dst, device_id_type=MESH)
    peers = 1 + sum(there.astype(jnp.int32) for there in (has_up, has_down, has_link))
    pl.semaphore_wait(barrier, peers)

    def remote(src, dst, ss, rs, target):
        return pltpu.make_async_remote_copy(
            src_ref=src, dst_ref=dst, send_sem=ss, recv_sem=rs,
            device_id=target, device_id_type=MESH,
        )

    def query_copies(side, slot_there, target, c):
        return (
            remote(q_in.at[:, cols(c)], qs.at[slot_there, :, cols(c)], q_ss.at[side - 1, 0, c], q_rs.at[slot_there - 1, 0, c], target),
            remote(g_in.at[:, cols(c)], gs.at[slot_there, :, cols(c)], q_ss.at[side - 1, 1, c], q_rs.at[slot_there - 1, 1, c], target),
        )

    def aux_copy(side, slot_there, target):
        return remote(aux.at[OWN], aux.at[slot_there], aux_ss.at[side - 1], aux_rs.at[slot_there - 1], target)

    def key_copies(slot, target, c):
        return (
            remote(k_in.at[:, cols(c)], ks.at[slot, :, cols(c)], kv_ss.at[slot - 1, 0, c], kv_rs.at[slot - 1, 0, c], target),
            remote(v_in.at[:, cols(c)], vs.at[slot, :, cols(c)], kv_ss.at[slot - 1, 1, c], kv_rs.at[slot - 1, 1, c], target),
        )

    def dq_copy(side, slot_there, target, c):
        return remote(
            dq_send.at[side - 1, :, cols(c)], dq_recv.at[slot_there - 1, :, cols(c)],
            dq_ss.at[side - 1, c], dq_rs.at[slot_there - 1, c], target,
        )

    def dkv_copies(slot, target, c):
        return (
            remote(dk_send.at[slot - 1, :, cols(c)], dk_recv.at[slot - 1, :, cols(c)], dkv_ss.at[slot - 1, 0, c], dkv_rs.at[slot - 1, 0, c], target),
            remote(dv_send.at[slot - 1, :, cols(c)], dv_recv.at[slot - 1, :, cols(c)], dkv_ss.at[slot - 1, 1, c], dkv_rs.at[slot - 1, 1, c], target),
        )

    def loop(first, last, body):
        def run(c, carry):
            body(c)
            return carry

        lax.fori_loop(first, last, run, 0)

    def start_queries(c):
        for there, target, side, slot_there in row_sides:
            @pl.when(there)
            def _():
                for copy in query_copies(side, slot_there, target, c):
                    copy.start()

    def start_keys(c):
        for copy in key_copies(CHIP, to_chip, c):
            copy.start()
        @pl.when(has_link)
        def _():
            for copy in key_copies(LINK, to_link, c):
                copy.start()

    loop(0, EARLY, start_queries)
    loop(0, chunks, start_keys)

    local[0].wait()
    local[1].wait()
    aux[OWN] = jnp.zeros((AUX_ROWS, tile), F32)
    aux[OWN, 0:heads, :] = lse_ref[...] * LOG2E
    ones = jnp.ones((8, width), LOW)

    def delta_row(h):
        products = gs[OWN, :, head_cols(h)].astype(F32) * outs[:, head_cols(h)].astype(F32)
        high = products.astype(LOW)
        low = (products - high.astype(F32)).astype(LOW)
        aux[OWN, pl.ds(DELTA_ROW + h, 1), :] = (dot(ones, high, NT) + dot(ones, low, NT))[0:1]

    loop(0, heads, delta_row)
    for i in range(9):
        if i == 4:
            line = jnp.zeros((1, tile), F32)
        else:
            line = jnp.where(jnp.full((1, tile), mask_ref[0, i], jnp.int32) > 0, 0.0, 1e30)
        aux[OWN, PEN_ROW + i : PEN_ROW + i + 1, :] = line
    for there, target, side, slot_there in row_sides:
        @pl.when(there)
        def _():
            aux_copy(side, slot_there, target).start()
    loop(EARLY, chunks, start_queries)

    for there, slot in ((has_up, UP), (has_down, DOWN)):
        @pl.when(jnp.logical_not(there))
        def _():
            qs[slot] = jnp.zeros((tile, full), LOW)
            gs[slot] = jnp.zeros((tile, full), LOW)
            aux[slot] = jnp.zeros((AUX_ROWS, tile), F32)

    for copy in local[2:]:
        copy.wait()
    for there, target, side, slot_there in row_sides:
        @pl.when(there)
        def _():
            aux_copy(slot_there, side, target).wait_recv()

    def pick(source, first, index):
        table = aux[source, first : first + 16, :]
        chosen = lax.broadcasted_iota(jnp.int32, table.shape, 0) == index
        return jnp.sum(jnp.where(chosen, table, 0.0), 0, keepdims=True)

    def pair_block(h, slot, offset):
        at = head_cols(h)
        q = qs[:, :, at].reshape(3 * tile, width)
        g = gs[:, :, at].reshape(3 * tile, width)
        k, v = ks[slot, :, at], vs[slot, :, at]
        lines, deltas = [], []
        for source, row_offset in ((OWN, 0), (UP, -1), (DOWN, 1)):
            pen = 3 * (offset + 1) + row_offset + 1
            lines.append(pick(source, 0, h) + pick(source, PEN_ROW, pen))
            deltas.append(pick(source, DELTA_ROW, h))
        line, delta = jnp.concatenate(lines, 1), jnp.concatenate(deltas, 1)
        weights = jnp.exp2(dot(k, q, NT) * (scale * LOG2E) - line)
        grad_score = (weights * (dot(v, g, NT) - delta)).astype(LOW)
        dk = dot(grad_score, q, NN) * scale
        dv = dot(weights.astype(LOW), g, NN)
        return dk, dv, dot(k, grad_score, TN)

    def finish_queries(h, total):
        at = head_cols(h)
        for source in (OWN, UP, DOWN):
            part = total[:, source * tile : (source + 1) * tile].T * scale
            if source == OWN:
                dq_own[:, at] = part
            else:
                dq_send[source - 1, :, at] = part.astype(LOW)

    def start_dq(c):
        for there, target, side, slot_there in row_sides:
            @pl.when(there)
            def _():
                dq_copy(side, slot_there, target, c).start()

    def first_pass(c):
        for there, target, side, slot_there in row_sides:
            @pl.when(there)
            def _():
                for copy in query_copies(slot_there, side, target, c):
                    copy.wait_recv()
        for copy in key_copies(CHIP, to_chip, c):
            copy.wait_recv()
        for i in range(GROUP):
            h = c * GROUP + i
            at = head_cols(h)
            dk, dv, total = pair_block(h, 0, 0)
            dk_own[:, at] = dk
            dv_own[:, at] = dv
            dk, dv, more = pair_block(h, CHIP, step)
            dk_send[CHIP - 1, :, at] = dk.astype(LOW)
            dv_send[CHIP - 1, :, at] = dv.astype(LOW)
            total = total + more
            dq_acc[h] = total
            @pl.when(jnp.logical_not(has_link))
            def _():
                finish_queries(h, dq_acc[h])
        for copy in dkv_copies(CHIP, to_chip, c):
            copy.start()
        @pl.when(jnp.logical_not(has_link))
        def _():
            start_dq(c)

    loop(0, chunks, first_pass)

    def second_pass(c):
        for copy in key_copies(LINK, to_link, c):
            copy.wait_recv()
        for i in range(GROUP):
            h = c * GROUP + i
            at = head_cols(h)
            dk, dv, more = pair_block(h, LINK, -step)
            dk_send[LINK - 1, :, at] = dk.astype(LOW)
            dv_send[LINK - 1, :, at] = dv.astype(LOW)
            finish_queries(h, dq_acc[h] + more)
        for copy in dkv_copies(LINK, to_link, c):
            copy.start()
        start_dq(c)

    @pl.when(has_link)
    def _():
        loop(0, chunks, second_pass)

    @pl.when(jnp.logical_not(has_link))
    def _():
        dk_recv[LINK - 1] = jnp.zeros((tile, full), LOW)
        dv_recv[LINK - 1] = jnp.zeros((tile, full), LOW)
    for there, slot in ((has_up, UP), (has_down, DOWN)):
        @pl.when(jnp.logical_not(there))
        def _():
            dq_recv[slot - 1] = jnp.zeros((tile, full), LOW)

    def last_pass(c):
        at = cols(c)
        for there, target, side, slot_there in row_sides:
            @pl.when(there)
            def _():
                dq_copy(slot_there, side, target, c).wait_recv()
        for copy in dkv_copies(CHIP, to_chip, c):
            copy.wait_recv()
        @pl.when(has_link)
        def _():
            for copy in dkv_copies(LINK, to_link, c):
                copy.wait_recv()
        for own, recv, out in ((dq_own, dq_recv, dq_out), (dk_own, dk_recv, dk_out), (dv_own, dv_recv, dv_out)):
            out[:, at] = (own[:, at] + recv[0, :, at].astype(F32) + recv[1, :, at].astype(F32)).astype(LOW)

    loop(0, chunks, last_pass)

    for there, target, side, slot_there in row_sides:
        @pl.when(there)
        def _():
            aux_copy(side, slot_there, target).wait_send()

    def drain(c):
        for there, target, side, slot_there in row_sides:
            @pl.when(there)
            def _():
                for copy in query_copies(side, slot_there, target, c):
                    copy.wait_send()
                dq_copy(side, slot_there, target, c).wait_send()
        for copy in key_copies(CHIP, to_chip, c) + dkv_copies(CHIP, to_chip, c):
            copy.wait_send()
        @pl.when(has_link)
        def _():
            for copy in key_copies(LINK, to_link, c) + dkv_copies(LINK, to_link, c):
                copy.wait_send()

    loop(0, chunks, drain)


def per_device(queries, keys, values, outputs, out_grads, log_sums, window_mask):
    shape = queries.shape
    tile, full = shape[2:]
    heads = log_sums.shape[2]
    width = full // heads
    chunks = heads // GROUP
    flat = (tile, full)
    any_spec = pl.BlockSpec(memory_space=pl.ANY)
    vmem = pl.BlockSpec(memory_space=pltpu.VMEM)
    dma = pltpu.SemaphoreType.DMA
    grads = pl.pallas_call(
        kernel,
        out_shape=(jax.ShapeDtypeStruct(flat, LOW),) * 3,
        in_specs=[any_spec] * 5 + [vmem, pl.BlockSpec(memory_space=pltpu.SMEM)],
        out_specs=(vmem,) * 3,
        scratch_shapes=[
            *[pltpu.VMEM((3,) + flat, LOW)] * 4,
            pltpu.VMEM(flat, LOW),
            pltpu.VMEM((3, AUX_ROWS, tile), F32),
            pltpu.VMEM((heads, width, 3 * tile), F32),
            *[pltpu.VMEM(flat, F32)] * 3,
            *[pltpu.VMEM((2,) + flat, LOW)] * 6,
            dma((5,)),
            dma((2, 2, chunks)), dma((2, 2, chunks)),
            dma((2, 2, chunks)), dma((2, 2, chunks)),
            dma((2,)), dma((2,)),
            dma((2, chunks)), dma((2, chunks)),
            dma((2, 2, chunks)), dma((2, 2, chunks)),
        ],
        compiler_params=pltpu.CompilerParams(
            collective_id=0, has_side_effects=True, vmem_limit_bytes=63 * 2**20
        ),
        name="tile_attention_backward",
    )(
        *[x.reshape(flat) for x in (queries, keys, values, outputs, out_grads)],
        log_sums.reshape(heads, tile),
        window_mask.reshape(1, -1),
    )
    return tuple(g.reshape(shape) for g in grads)


def solution(mesh):
    tiles = P("tm", "space", None, None)
    return jax.shard_map(
        per_device,
        mesh=mesh,
        in_specs=(tiles,) * 6 + (P("tm", "space", None),),
        out_specs=(tiles,) * 3,
        check_vma=False,
    )
```

time: 585 us -> 161 us (0.28)
  the two profiles are of different devices: /device:TPU:5 before, /device:TPU:26 now
where the time goes in v1:
time: 161 us
  Pallas kernels  154 us (96%)
  local copies, waits for them, and re-layouts  6.5 us (4%)
    pallas_call x1, Pallas kernels, per_device(): pl.pallas_call(kernel, out_shape=(jax.ShapeDtypeStruct(flat, LOW),) * 3,...  154 us
    unnamed x8, local copies, waits for them, and re-layouts  6.5 us

profile of v1, /device:TPU:26, one launch (start us, length us, event | category | flops | bytes accessed | tf_op | source)
XLA Modules:
  0.0 160.8 jit_solution(16284442071374191329)
XLA Ops:
  0.6 1.3 copy.12
  2.0 153.7 %tile_attention_backward.1 = (bf16[384,1536]{1,0:T(8,128)(2,1)}, bf16[384,1536]{1,0:T(8,128)(2,1)}, bf16[384,1536]{1,0:T(8,128)(2,1)}) custom-call(bf16[384,1536]{1,0:T(8,128)(2,1)} %bitcast.15, bf16[384,1536]{1,0:T(8,128)(2,1)} %bitcast.16, bf16[384,1536]{1,0:T(8,128)(2,1)} %bitcast.17, bf16[384,1536]{1,0:T(8,128)(2,1)} %bitcast.18, ...), custom_call_target="tpu_custom_call" | custom-call | tf_op jit(solution)/shard_map/tile_attention_backward/pallas_call | solution.py:317
  155.6 0.0 copy-start.1
  155.6 2.5 %copy.16 = bf16[1,1,384,1536]{3,2,1,0:T(8,128)(2,1)} copy(bf16[1,1,384,1536]{3,2,1,0:T(8,128)(2,1)} %bitcast.14) | data formatting | bytes 2359296
  158.1 0.0 copy-done.1
  158.1 0.0 copy-start
  158.1 1.0 copy.17
  159.1 0.7 copy-done
  159.8 1.0 copy.18
Async XLA Ops:
  155.6 2.5 %copy-start.1 = (bf16[384,1536]{1,0:T(8,128)(2,1)S(1)}, bf16[384,1536]{1,0:T(8,128)(2,1)}, u32[]{:S(2)}) copy-start(bf16[384,1536]{1,0:T(8,128)(2,1)} %get-tuple-element.7) | copy-start | bytes 3538948
  158.1 1.7 %copy-start = (bf16[384,1536]{1,0:T(8,128)(2,1)S(1)}, bf16[384,1536]{1,0:T(8,128)(2,1)}, u32[]{:S(2)}) copy-start(bf16[384,1536]{1,0:T(8,128)(2,1)} %get-tuple-element.8) | copy-start | bytes 3538948

commit v2 on v1

--- a/solution.py
+++ b/solution.py
@@ -20,6 +20,7 @@
 OWN, UP, DOWN = 0, 1, 2
 CHIP, LINK = 1, 2
 DELTA_ROW, PEN_ROW, AUX_ROWS = 16, 32, 48
+RELAYED = 6
 
 
 def dot(a, b, dims):
@@ -30,8 +31,8 @@
     q_in, k_in, v_in, o_in, g_in, lse_ref, mask_ref,
     dq_out, dk_out, dv_out,
     qs, gs, ks, vs, outs, aux, dq_acc, dq_own, dk_own, dv_own,
-    dq_send, dk_send, dv_send, dq_recv, dk_recv, dv_recv,
-    in_sem, q_ss, q_rs, kv_ss, kv_rs, aux_ss, aux_rs, dq_ss, dq_rs, dkv_ss, dkv_rs,
+    dq_send, dk_send, dv_send, dq_recv, dk_recv, dv_recv, passing,
+    in_sem, pass_rs, pass_ss, q_ss, q_rs, kv_ss, kv_rs, aux_ss, aux_rs, dq_ss, dq_rs, dkv_ss, dkv_rs,
 ):
     tile, full = q_in.shape
     heads = lse_ref.shape[0]
@@ -48,6 +49,12 @@
     has_link = jnp.logical_and(other >= 0, other < frames)
     to_up, to_down = (frame, row + 1), (frame, row - 1)
     to_chip, to_link = (frame + step, row), (other, row)
+    place = lax.rem(row, 4)
+    partner = row + 1 - 2 * lax.rem(place, 2)
+    is_outer = jnp.logical_or(place == 0, place == 3)
+    via = jnp.logical_and(has_link, is_outer)
+    carries = jnp.logical_and(has_link, jnp.logical_not(is_outer))
+    to_partner, to_cross = (frame, partner), (other, partner)
     row_sides = ((has_up, to_up, UP, DOWN), (has_down, to_down, DOWN, UP))
 
     def cols(c):
@@ -67,11 +74,11 @@
 
     barrier = pltpu.get_barrier_semaphore()
     pl.semaphore_signal(barrier, inc=1, device_id=to_chip, device_id_type=MESH)
-    for there, dst in ((has_up, to_up), (has_down, to_down), (has_link, to_link)):
+    for there, dst in ((has_up, to_up), (has_down, to_down), (has_link, to_link), (has_link, to_cross)):
         @pl.when(there)
         def _():
             pl.semaphore_signal(barrier, inc=1, device_id=dst, device_id_type=MESH)
-    peers = 1 + sum(there.astype(jnp.int32) for there in (has_up, has_down, has_link))
+    peers = 1 + sum(there.astype(jnp.int32) for there in (has_up, has_down, has_link, has_link))
     pl.semaphore_wait(barrier, peers)
 
     def remote(src, dst, ss, rs, target):
@@ -107,6 +114,26 @@
             remote(dv_send.at[slot - 1, :, cols(c)], dv_recv.at[slot - 1, :, cols(c)], dkv_ss.at[slot - 1, 1, c], dkv_rs.at[slot - 1, 1, c], target),
         )
 
+    def via_copies(kind, c):
+        sources, ss = (((k_in, v_in), kv_ss), ((dk_send.at[LINK - 1], dv_send.at[LINK - 1]), dkv_ss))[kind]
+        return [
+            remote(src.at[:, cols(c)], passing.at[kind, i, :, cols(c)], ss.at[LINK - 1, i, c], pass_rs.at[kind, i, c], to_partner)
+            for i, src in enumerate(sources)
+        ]
+
+    def onward_copies(kind, c):
+        targets, rs = (((ks.at[LINK], vs.at[LINK]), kv_rs), ((dk_recv.at[LINK - 1], dv_recv.at[LINK - 1]), dkv_rs))[kind]
+        return [
+            remote(passing.at[kind, i, :, cols(c)], dst.at[:, cols(c)], pass_ss.at[kind, i, c], rs.at[LINK - 1, i, c], to_cross)
+            for i, dst in enumerate(targets)
+        ]
+
+    def carry(kind, c):
+        for copy in via_copies(kind, c):
+            copy.wait_recv()
+        for copy in onward_copies(kind, c):
+            copy.start()
+
     def loop(first, last, body):
         def run(c, carry):
             body(c)
@@ -120,11 +147,15 @@
             def _():
                 for copy in query_copies(side, slot_there, target, c):
                     copy.start()
+        @pl.when(jnp.logical_and(via, jnp.logical_and(lax.rem(c, 2) == 1, c // 2 < RELAYED)))
+        def _():
+            for copy in via_copies(0, c // 2):
+                copy.start()
 
     def start_keys(c):
         for copy in key_copies(CHIP, to_chip, c):
             copy.start()
-        @pl.when(has_link)
+        @pl.when(jnp.logical_and(has_link, jnp.logical_or(c >= RELAYED, carries)))
         def _():
             for copy in key_copies(LINK, to_link, c):
                 copy.start()
@@ -216,6 +247,9 @@
                     copy.wait_recv()
         for copy in key_copies(CHIP, to_chip, c):
             copy.wait_recv()
+        @pl.when(jnp.logical_and(carries, jnp.logical_and(lax.rem(c, 2) == 0, c >= 2)))
+        def _():
+            carry(0, c // 2 - 1)
         for i in range(GROUP):
             h = c * GROUP + i
             at = head_cols(h)
@@ -238,6 +272,10 @@
 
     loop(0, chunks, first_pass)
 
+    @pl.when(carries)
+    def _():
+        carry(0, RELAYED - 1)
+
     def second_pass(c):
         for copy in key_copies(LINK, to_link, c):
             copy.wait_recv()
@@ -248,13 +286,24 @@
             dk_send[LINK - 1, :, at] = dk.astype(LOW)
             dv_send[LINK - 1, :, at] = dv.astype(LOW)
             finish_queries(h, dq_acc[h] + more)
-        for copy in dkv_copies(LINK, to_link, c):
-            copy.start()
+        relayed = jnp.logical_and(is_outer, c < RELAYED)
+        @pl.when(relayed)
+        def _():
+            for copy in via_copies(1, c):
+                copy.start()
+        @pl.when(jnp.logical_not(relayed))
+        def _():
+            for copy in dkv_copies(LINK, to_link, c):
+                copy.start()
         start_dq(c)
 
     @pl.when(has_link)
     def _():
         loop(0, chunks, second_pass)
+
+    @pl.when(carries)
+    def _():
+        loop(0, RELAYED, lambda c: carry(1, c))
 
     @pl.when(jnp.logical_not(has_link))
     def _():
@@ -302,6 +351,15 @@
                 copy.wait_send()
 
     loop(0, chunks, drain)
+
+    def drain_carried(c):
+        for kind in (0, 1):
+            for copy in onward_copies(kind, c):
+                copy.wait_send()
+
+    @pl.when(carries)
+    def _():
+        loop(0, RELAYED, drain_carried)
 
 
 def per_device(queries, keys, values, outputs, out_grads, log_sums, window_mask):
@@ -326,7 +384,8 @@
             pltpu.VMEM((heads, width, 3 * tile), F32),
             *[pltpu.VMEM(flat, F32)] * 3,
             *[pltpu.VMEM((2,) + flat, LOW)] * 6,
-            dma((5,)),
+            pltpu.VMEM((2, 2, tile, RELAYED * GROUP * width), LOW),
+            dma((5,)), dma((2, 2, RELAYED)), dma((2, 2, RELAYED)),
             dma((2, 2, chunks)), dma((2, 2, chunks)),
             dma((2, 2, chunks)), dma((2, 2, chunks)),
             dma((2,)), dma((2,)),

time: 161 us -> 144 us (0.89)
  the two profiles are of different devices: /device:TPU:26 before, /device:TPU:5 now
where the time goes in v2:
time: 144 us; the launch traced here: 143 us
  Pallas kernels  136 us (94%)
  local copies, waits for them, and re-layouts  6.5 us (5%)
    pallas_call x1, Pallas kernels, per_device(): pl.pallas_call(kernel, out_shape=(jax.ShapeDtypeStruct(flat, LOW),) * 3,...  136 us
    unnamed x8, local copies, waits for them, and re-layouts  6.5 us

profile of v2, /device:TPU:5, one launch (start us, length us, event | category | flops | bytes accessed | tf_op | source)
XLA Modules:
  0.0 143.2 jit_solution(6417386518614812776)
XLA Ops:
  0.6 1.3 copy.12
  2.0 136.0 %tile_attention_backward.1 = (bf16[384,1536]{1,0:T(8,128)(2,1)}, bf16[384,1536]{1,0:T(8,128)(2,1)}, bf16[384,1536]{1,0:T(8,128)(2,1)}) custom-call(bf16[384,1536]{1,0:T(8,128)(2,1)} %bitcast.15, bf16[384,1536]{1,0:T(8,128)(2,1)} %bitcast.16, bf16[384,1536]{1,0:T(8,128)(2,1)} %bitcast.17, bf16[384,1536]{1,0:T(8,128)(2,1)} %bitcast.18, ...), custom_call_target="tpu_custom_call" | custom-call | tf_op jit(solution)/shard_map/tile_attention_backward/pallas_call | solution.py:375
  138.0 0.0 copy-start.1
  138.0 2.5 %copy.16 = bf16[1,1,384,1536]{3,2,1,0:T(8,128)(2,1)} copy(bf16[1,1,384,1536]{3,2,1,0:T(8,128)(2,1)} %bitcast.14) | data formatting | bytes 2359296
  140.4 0.0 copy-done.1
  140.4 0.0 copy-start
  140.4 1.0 copy.17
  141.5 0.7 copy-done
  142.1 1.0 copy.18
Async XLA Ops:
  138.0 2.5 %copy-start.1 = (bf16[384,1536]{1,0:T(8,128)(2,1)S(1)}, bf16[384,1536]{1,0:T(8,128)(2,1)}, u32[]{:S(2)}) copy-start(bf16[384,1536]{1,0:T(8,128)(2,1)} %get-tuple-element.7) | copy-start | bytes 3538948
  140.4 1.7 %copy-start = (bf16[384,1536]{1,0:T(8,128)(2,1)S(1)}, bf16[384,1536]{1,0:T(8,128)(2,1)}, u32[]{:S(2)}) copy-start(bf16[384,1536]{1,0:T(8,128)(2,1)} %get-tuple-element.8) | copy-start | bytes 3538948

commit v3 on v2

--- a/solution.py
+++ b/solution.py
@@ -20,7 +20,9 @@
 OWN, UP, DOWN = 0, 1, 2
 CHIP, LINK = 1, 2
 DELTA_ROW, PEN_ROW, AUX_ROWS = 16, 32, 48
-RELAYED = 6
+VIA_KEYS = 12
+VIA_GRADS = 0
+LEAD = 3
 
 
 def dot(a, b, dims):
@@ -30,7 +32,7 @@
 def kernel(
     q_in, k_in, v_in, o_in, g_in, lse_ref, mask_ref,
     dq_out, dk_out, dv_out,
-    qs, gs, ks, vs, outs, aux, dq_acc, dq_own, dk_own, dv_own,
+    qs, gs, ks, vs, outs, aux, dq_sum, dq_own, dk_own, dv_own,
     dq_send, dk_send, dv_send, dq_recv, dk_recv, dv_recv, passing,
     in_sem, pass_rs, pass_ss, q_ss, q_rs, kv_ss, kv_rs, aux_ss, aux_rs, dq_ss, dq_rs, dkv_ss, dkv_rs,
 ):
@@ -142,26 +144,34 @@
         lax.fori_loop(first, last, run, 0)
 
     def start_queries(c):
+        @pl.when(jnp.logical_and(via, c < VIA_KEYS))
+        def _():
+            for copy in via_copies(0, c):
+                copy.start()
         for there, target, side, slot_there in row_sides:
             @pl.when(there)
             def _():
                 for copy in query_copies(side, slot_there, target, c):
                     copy.start()
-        @pl.when(jnp.logical_and(via, jnp.logical_and(lax.rem(c, 2) == 1, c // 2 < RELAYED)))
-        def _():
-            for copy in via_copies(0, c // 2):
-                copy.start()
 
     def start_keys(c):
         for copy in key_copies(CHIP, to_chip, c):
             copy.start()
-        @pl.when(jnp.logical_and(has_link, jnp.logical_or(c >= RELAYED, carries)))
-        def _():
-            for copy in key_copies(LINK, to_link, c):
-                copy.start()
+
+    def start_link_keys(c):
+        for copy in key_copies(LINK, to_link, c):
+            copy.start()
 
     loop(0, EARLY, start_queries)
     loop(0, chunks, start_keys)
+
+    @pl.when(carries)
+    def _():
+        loop(0, LEAD, start_link_keys)
+
+    @pl.when(via)
+    def _():
+        loop(VIA_KEYS, chunks, start_link_keys)
 
     local[0].wait()
     local[1].wait()
@@ -239,17 +249,23 @@
             def _():
                 dq_copy(side, slot_there, target, c).start()
 
-    def first_pass(c):
+    def compute(c):
         for there, target, side, slot_there in row_sides:
             @pl.when(there)
             def _():
                 for copy in query_copies(slot_there, side, target, c):
                     copy.wait_recv()
+
+        @pl.when(jnp.logical_and(carries, c < VIA_KEYS))
+        def _():
+            carry(0, c)
+
+        @pl.when(jnp.logical_and(carries, c + LEAD < chunks))
+        def _():
+            start_link_keys(c + LEAD)
+
         for copy in key_copies(CHIP, to_chip, c):
             copy.wait_recv()
-        @pl.when(jnp.logical_and(carries, jnp.logical_and(lax.rem(c, 2) == 0, c >= 2)))
-        def _():
-            carry(0, c // 2 - 1)
         for i in range(GROUP):
             h = c * GROUP + i
             at = head_cols(h)
@@ -259,51 +275,39 @@
             dk, dv, more = pair_block(h, CHIP, step)
             dk_send[CHIP - 1, :, at] = dk.astype(LOW)
             dv_send[CHIP - 1, :, at] = dv.astype(LOW)
-            total = total + more
-            dq_acc[h] = total
-            @pl.when(jnp.logical_not(has_link))
-            def _():
-                finish_queries(h, dq_acc[h])
-        for copy in dkv_copies(CHIP, to_chip, c):
-            copy.start()
-        @pl.when(jnp.logical_not(has_link))
-        def _():
-            start_dq(c)
-
-    loop(0, chunks, first_pass)
+            dq_sum[...] = total + more
+            if i == GROUP - 1:
+                for copy in dkv_copies(CHIP, to_chip, c):
+                    copy.start()
+
+            @pl.when(has_link)
+            def _():
+                if i == 0:
+                    for copy in key_copies(LINK, to_link, c):
+                        copy.wait_recv()
+                dk, dv, more = pair_block(h, LINK, -step)
+                dk_send[LINK - 1, :, at] = dk.astype(LOW)
+                dv_send[LINK - 1, :, at] = dv.astype(LOW)
+                dq_sum[...] += more
+
+            finish_queries(h, dq_sum[...])
+
+        start_dq(c)
+        relayed = jnp.logical_and(is_outer, c < VIA_GRADS)
+        @pl.when(jnp.logical_and(has_link, relayed))
+        def _():
+            for copy in via_copies(1, c):
+                copy.start()
+        @pl.when(jnp.logical_and(has_link, jnp.logical_not(relayed)))
+        def _():
+            for copy in dkv_copies(LINK, to_link, c):
+                copy.start()
+
+    loop(0, chunks, compute)
 
     @pl.when(carries)
     def _():
-        carry(0, RELAYED - 1)
-
-    def second_pass(c):
-        for copy in key_copies(LINK, to_link, c):
-            copy.wait_recv()
-        for i in range(GROUP):
-            h = c * GROUP + i
-            at = head_cols(h)
-            dk, dv, more = pair_block(h, LINK, -step)
-            dk_send[LINK - 1, :, at] = dk.astype(LOW)
-            dv_send[LINK - 1, :, at] = dv.astype(LOW)
-            finish_queries(h, dq_acc[h] + more)
-        relayed = jnp.logical_and(is_outer, c < RELAYED)
-        @pl.when(relayed)
-        def _():
-            for copy in via_copies(1, c):
-                copy.start()
-        @pl.when(jnp.logical_not(relayed))
-        def _():
-            for copy in dkv_copies(LINK, to_link, c):
-                copy.start()
-        start_dq(c)
-
-    @pl.when(has_link)
-    def _():
-        loop(0, chunks, second_pass)
-
-    @pl.when(carries)
-    def _():
-        loop(0, RELAYED, lambda c: carry(1, c))
+        loop(0, VIA_GRADS, lambda c: carry(1, c))
 
     @pl.when(jnp.logical_not(has_link))
     def _():
@@ -352,14 +356,17 @@
 
     loop(0, chunks, drain)
 
-    def drain_carried(c):
-        for kind in (0, 1):
+    def drain_carried(kind):
+        def run(c):
             for copy in onward_copies(kind, c):
                 copy.wait_send()
 
+        return run
+
     @pl.when(carries)
     def _():
-        loop(0, RELAYED, drain_carried)
+        loop(0, VIA_KEYS, drain_carried(0))
+        loop(0, VIA_GRADS, drain_carried(1))
 
 
 def per_device(queries, keys, values, outputs, out_grads, log_sums, window_mask):
@@ -381,11 +388,11 @@
             *[pltpu.VMEM((3,) + flat, LOW)] * 4,
             pltpu.VMEM(flat, LOW),
             pltpu.VMEM((3, AUX_ROWS, tile), F32),
-            pltpu.VMEM((heads, width, 3 * tile), F32),
+            pltpu.VMEM((width, 3 * tile), F32),
             *[pltpu.VMEM(flat, F32)] * 3,
             *[pltpu.VMEM((2,) + flat, LOW)] * 6,
-            pltpu.VMEM((2, 2, tile, RELAYED * GROUP * width), LOW),
-            dma((5,)), dma((2, 2, RELAYED)), dma((2, 2, RELAYED)),
+            pltpu.VMEM((2, 2) + flat, LOW),
+            dma((5,)), dma((2, 2, chunks)), dma((2, 2, chunks)),
             dma((2, 2, chunks)), dma((2, 2, chunks)),
             dma((2, 2, chunks)), dma((2, 2, chunks)),
             dma((2,)), dma((2,)),

time: 144 us -> 127 us (0.88)
  Pallas kernels: 136 us -> 119 us
    pallas_call x1, Pallas kernels: 136 us -> 119 us  [per_device(): pl.pallas_call(kernel, out_shape=(jax.ShapeDtypeStruct(flat, LOW),) * 3,...]
where the time goes in v3:
time: 127 us; the launch traced here: 126 us
  Pallas kernels  119 us (94%)
  local copies, waits for them, and re-layouts  6.5 us (5%)
    pallas_call x1, Pallas kernels, per_device(): pl.pallas_call(kernel, out_shape=(jax.ShapeDtypeStruct(flat, LOW),) * 3,...  119 us
    unnamed x8, local copies, waits for them, and re-layouts  6.5 us

profile of v3, /device:TPU:5, one launch (start us, length us, event | category | flops | bytes accessed | tf_op | source)
XLA Modules:
  0.0 126.4 jit_solution(13530456234487883878)
XLA Ops:
  0.6 1.3 %copy.12 = f32[1,1,12,384]{3,2,1,0:T(8,128)} copy(f32[1,1,12,384]{3,1,2,0:T(1,128)} %param.12) | data formatting | bytes 36864
  2.0 119.2 %tile_attention_backward.1 = (bf16[384,1536]{1,0:T(8,128)(2,1)}, bf16[384,1536]{1,0:T(8,128)(2,1)}, bf16[384,1536]{1,0:T(8,128)(2,1)}) custom-call(bf16[384,1536]{1,0:T(8,128)(2,1)} %bitcast.15, bf16[384,1536]{1,0:T(8,128)(2,1)} %bitcast.16, bf16[384,1536]{1,0:T(8,128)(2,1)} %bitcast.17, bf16[384,1536]{1,0:T(8,128)(2,1)} %bitcast.18, ...), custom_call_target="tpu_custom_call" | custom-call | tf_op jit(solution)/shard_map/tile_attention_backward/pallas_call | solution.py:382
  121.2 0.0 copy-start.1
  121.2 2.5 %copy.16 = bf16[1,1,384,1536]{3,2,1,0:T(8,128)(2,1)} copy(bf16[1,1,384,1536]{3,2,1,0:T(8,128)(2,1)} %bitcast.14) | data formatting | bytes 2359296
  123.7 0.0 copy-done.1
  123.7 0.0 copy-start
  123.7 1.0 copy.17
  124.7 0.7 copy-done
  125.4 1.0 copy.18
Async XLA Ops:
  121.2 2.5 %copy-start.1 = (bf16[384,1536]{1,0:T(8,128)(2,1)S(1)}, bf16[384,1536]{1,0:T(8,128)(2,1)}, u32[]{:S(2)}) copy-start(bf16[384,1536]{1,0:T(8,128)(2,1)} %get-tuple-element.7) | copy-start | bytes 3538948
  123.7 1.7 %copy-start = (bf16[384,1536]{1,0:T(8,128)(2,1)S(1)}, bf16[384,1536]{1,0:T(8,128)(2,1)}, u32[]{:S(2)}) copy-start(bf16[384,1536]{1,0:T(8,128)(2,1)} %get-tuple-element.8) | copy-start | bytes 3538948

commit v4 on v3

v4 whole, which is shorter than its diff:
```python
import functools
import math

import jax
import jax.numpy as jnp
from jax import lax
from jax.experimental import pallas as pl
from jax.experimental.pallas import tpu as pltpu
from jax.sharding import PartitionSpec as P

F32 = jnp.float32
LOW = jnp.bfloat16
MESH = pl.DeviceIdType.MESH
EARLY = 2
LOG2E = math.log2(math.e)
NT = (((1,), (1,)), ((), ()))
NN = (((1,), (0,)), ((), ()))
TN = (((0,), (0,)), ((), ()))
OWN, NEAR, ACROSS = 0, 1, 2
CHIP, LINK, FAR = 1, 2, 3
DELTA_ROW, PEN_ROW, AUX_ROWS = 12, 24, 40
VIA_KEYS = 3
VIA_GRADS = 0
LEAD = 3


def dot(a, b, dims):
    return lax.dot_general(a, b, dims, preferred_element_type=F32)


def kernel(
    q_in, k_in, v_in, o_in, g_in, lse_ref, mask_ref,
    dq_out, dk_out, dv_out,
    qs, gs, ks, vs, outs, aux, dq_sum, held, dq_own, dk_own, dv_own,
    dq_send, dk_send, dv_send, dq_recv, dk_recv, dv_recv, passing,
    in_sem, pass_rs, pass_ss, q_ss, q_rs, kv_ss, kv_rs, aux_ss, aux_rs, dq_ss, dq_rs, dkv_ss, dkv_rs,
):
    tile, full = q_in.shape
    heads = lse_ref.shape[0]
    width = full // heads
    wide, chunks = width, heads
    scale = width**-0.5
    frame, row = lax.axis_index("tm"), lax.axis_index("space")
    frames, rows = lax.axis_size("tm"), lax.axis_size("space")
    odd = lax.rem(frame, 2)
    step = 1 - 2 * odd
    place = lax.rem(row, 4)
    toward = 1 - 2 * lax.rem(place, 2)
    partner, beyond = row + toward, row - toward
    outer = jnp.logical_or(place == 0, place == 3)
    inner = jnp.logical_not(outer)
    other = frames - 1 - frame
    middle = jnp.abs(other - frame) == 1
    has_link = jnp.logical_or(outer, middle)
    has_across = jnp.logical_and(beyond >= 0, beyond < rows)
    across_frame = jnp.where(outer, other, frame)
    to_near, to_across = (frame, partner), (across_frame, beyond)
    to_chip, to_link, to_cross = (frame + step, row), (other, row), (other, partner)
    key_frames = (frame, frame + step, other, frames - 1 - (frame + step))
    query_frames = ((frame, 0), (frame, -toward), (across_frame, toward))

    def cols(c):
        return pl.ds(pl.multiple_of(c * wide, wide), wide)

    def head_cols(h):
        return pl.ds(pl.multiple_of(h * width, width), width)

    local = [
        pltpu.make_async_copy(src, dst, in_sem.at[i])
        for i, (src, dst) in enumerate(
            ((o_in, outs), (g_in, gs.at[OWN]), (q_in, qs.at[OWN]), (k_in, ks.at[0]), (v_in, vs.at[0]))
        )
    ]
    for copy in local:
        copy.start()

    barrier = pltpu.get_barrier_semaphore()
    pl.semaphore_signal(barrier, inc=1, device_id=to_chip, device_id_type=MESH)
    pl.semaphore_signal(barrier, inc=1, device_id=to_near, device_id_type=MESH)
    for there, dst in ((has_across, to_across), (has_link, to_link)):
        @pl.when(there)
        def _():
            pl.semaphore_signal(barrier, inc=1, device_id=dst, device_id_type=MESH)
    pl.semaphore_signal(barrier, inc=1, device_id=to_cross, device_id_type=MESH)
    peers = 3 + has_across.astype(jnp.int32) + has_link.astype(jnp.int32)
    pl.semaphore_wait(barrier, peers)

    def remote(src, dst, ss, rs, target):
        return pltpu.make_async_remote_copy(
            src_ref=src, dst_ref=dst, send_sem=ss, recv_sem=rs,
            device_id=target, device_id_type=MESH,
        )

    def query_copies(slot, c):
        target = to_near if slot == NEAR else to_across
        return [
            remote(src.at[:, cols(c)], dst.at[slot, :, cols(c)], q_ss.at[slot - 1, i, c], q_rs.at[slot - 1, i, c], target)
            for i, (src, dst) in enumerate(((q_in, qs), (g_in, gs)))
        ]

    def aux_copy(slot):
        target = to_near if slot == NEAR else to_across
        return remote(aux.at[OWN], aux.at[slot], aux_ss.at[slot - 1], aux_rs.at[slot - 1], target)

    def key_copies(slot, target, c):
        sources = (ks.at[LINK], vs.at[LINK]) if slot == FAR else (k_in, v_in)
        return [
            remote(src.at[:, cols(c)], dst.at[slot, :, cols(c)], kv_ss.at[slot - 1, i, c], kv_rs.at[slot - 1, i, c], target)
            for i, (src, dst) in enumerate(zip(sources, (ks, vs)))
        ]

    def dq_copy(slot, c):
        target = to_near if slot == NEAR else to_across
        return remote(
            dq_send.at[slot - 1, :, cols(c)], dq_recv.at[slot - 1, :, cols(c)],
            dq_ss.at[slot - 1, c], dq_rs.at[slot - 1, c], target,
        )

    def dkv_copies(slot, target, c):
        return (
            remote(dk_send.at[slot - 1, :, cols(c)], dk_recv.at[slot - 1, :, cols(c)], dkv_ss.at[slot - 1, 0, c], dkv_rs.at[slot - 1, 0, c], target),
            remote(dv_send.at[slot - 1, :, cols(c)], dv_recv.at[slot - 1, :, cols(c)], dkv_ss.at[slot - 1, 1, c], dkv_rs.at[slot - 1, 1, c], target),
        )

    def via_copies(kind, c):
        sources, ss = (((k_in, v_in), kv_ss), ((dk_send.at[LINK - 1], dv_send.at[LINK - 1]), dkv_ss))[kind]
        return [
            remote(src.at[:, cols(c)], passing.at[kind, i, :, cols(c)], ss.at[LINK - 1, i, c], pass_rs.at[kind, i, c], to_near)
            for i, src in enumerate(sources)
        ]

    def onward_copies(kind, c):
        targets, rs = (((ks.at[LINK], vs.at[LINK]), kv_rs), ((dk_recv.at[LINK - 1], dv_recv.at[LINK - 1]), dkv_rs))[kind]
        return [
            remote(passing.at[kind, i, :, cols(c)], dst.at[:, cols(c)], pass_ss.at[kind, i, c], rs.at[LINK - 1, i, c], to_cross)
            for i, dst in enumerate(targets)
        ]

    def carry(kind, c):
        for copy in via_copies(kind, c):
            copy.wait_recv()
        for copy in onward_copies(kind, c):
            copy.start()

    def loop(first, last, body):
        def run(c, carry):
            body(c)
            return carry

        lax.fori_loop(first, last, run, 0)

    def start_queries(c):
        @pl.when(jnp.logical_and(outer, c < VIA_KEYS))
        def _():
            for copy in via_copies(0, c):
                copy.start()
        for copy in query_copies(NEAR, c):
            copy.start()

        @pl.when(has_across)
        def _():
            for copy in query_copies(ACROSS, c):
                copy.start()

    def start_keys(c):
        for copy in key_copies(CHIP, to_chip, c):
            copy.start()

    def start_link_keys(c):
        for copy in key_copies(LINK, to_link, c):
            copy.start()

    loop(0, EARLY, start_queries)
    loop(0, chunks, start_keys)

    @pl.when(jnp.logical_and(inner, has_link))
    def _():
        loop(0, LEAD, start_link_keys)

    @pl.when(outer)
    def _():
        loop(VIA_KEYS, chunks, start_link_keys)

    local[0].wait()
    local[1].wait()
    aux[OWN] = jnp.zeros((AUX_ROWS, tile), F32)
    for h in range(heads):
        aux[OWN, h : h + 1, :] = lse_ref[h] * LOG2E
    ones = jnp.ones((8, width), LOW)

    def delta_row(h):
        products = gs[OWN, :, head_cols(h)].astype(F32) * outs[:, head_cols(h)].astype(F32)
        high = products.astype(LOW)
        low = (products - high.astype(F32)).astype(LOW)
        aux[OWN, pl.ds(DELTA_ROW + h, 1), :] = (dot(ones, high, NT) + dot(ones, low, NT))[0:1]

    loop(0, heads, delta_row)
    for i in range(9):
        if i == 4:
            line = jnp.zeros((1, tile), F32)
        else:
            line = jnp.where(jnp.full((1, tile), mask_ref[0, i], jnp.int32) > 0, 0.0, 1e30)
        aux[OWN, PEN_ROW + i : PEN_ROW + i + 1, :] = line
    aux_copy(NEAR).start()

    @pl.when(has_across)
    def _():
        aux_copy(ACROSS).start()

    loop(EARLY, chunks, start_queries)

    @pl.when(jnp.logical_not(has_across))
    def _():
        qs[ACROSS] = jnp.zeros((tile, full), LOW)
        gs[ACROSS] = jnp.zeros((tile, full), LOW)
        aux[ACROSS] = jnp.zeros((AUX_ROWS, tile), F32)

    for copy in local[2:]:
        copy.wait()
    aux_copy(NEAR).wait_recv()

    @pl.when(has_across)
    def _():
        aux_copy(ACROSS).wait_recv()

    def pick(table, index):
        chosen = lax.broadcasted_iota(jnp.int32, table.shape, 0) == index
        return jnp.sum(jnp.where(chosen, table, 0.0), 0, keepdims=True)

    def pair_block(h, slot, sources, fresh=False):
        at = head_cols(h)
        first, count = sources[0], len(sources)
        q = qs[first : first + count, :, at].reshape(count * tile, width)
        g = gs[first : first + count, :, at].reshape(count * tile, width)
        k, v = ks[slot, :, at], vs[slot, :, at]
        lines, deltas = [], []
        for source in sources:
            query_frame, row_offset = query_frames[source]
            table = aux[source]
            pen = PEN_ROW + 3 * (key_frames[slot] - query_frame + 1) + row_offset + 1
            lines.append(pick(table, h) + pick(table, pen))
            deltas.append(pick(table, DELTA_ROW + h))
        line, delta = jnp.concatenate(lines, 1), jnp.concatenate(deltas, 1)
        weights = jnp.exp2(dot(k, q, NT) * (scale * LOG2E) - line)
        grad_score = (weights * (dot(v, g, NT) - delta)).astype(LOW)
        span = slice(first * tile, (first + count) * tile)
        more = dot(k, grad_score, TN)
        dq_sum[:, span] = more if fresh else dq_sum[:, span] + more
        return dot(grad_score, q, NN) * scale, dot(weights.astype(LOW), g, NN)

    ALL, PAIR, LAST = (OWN, NEAR, ACROSS), (OWN, NEAR), (ACROSS,)

    def either(condition, body, yes, no):
        @pl.when(condition)
        def _():
            body(yes)

        @pl.when(jnp.logical_not(condition))
        def _():
            body(no)

    def finish_queries(h):
        at = head_cols(h)
        for source in (OWN, NEAR, ACROSS):
            part = dq_sum[:, source * tile : (source + 1) * tile].T * scale
            if source == OWN:
                dq_own[:, at] = part
            else:
                dq_send[source - 1, :, at] = part.astype(LOW)

    def start_dq(c):
        dq_copy(NEAR, c).start()

        @pl.when(has_across)
        def _():
            dq_copy(ACROSS, c).start()

    def send_link_grads(c):
        relayed = jnp.logical_and(outer, c < VIA_GRADS)

        @pl.when(relayed)
        def _():
            for copy in via_copies(1, c):
                copy.start()

        @pl.when(jnp.logical_not(relayed))
        def _():
            for copy in dkv_copies(LINK, to_link, c):
                copy.start()

    def merge(c):
        at = head_cols(c)
        for copy in dkv_copies(FAR, to_chip, c):
            copy.wait_recv()
        for i, (recv, send) in enumerate(((dk_recv, dk_send), (dv_recv, dv_send))):
            total = held[lax.rem(c, 2), i] + recv[FAR - 1, :, at].astype(F32)
            send[LINK - 1, :, at] = total.astype(LOW)
        send_link_grads(c)

    def compute(h):
        at = head_cols(h)
        for copy in query_copies(NEAR, h):
            copy.wait_recv()

        @pl.when(has_across)
        def _():
            for copy in query_copies(ACROSS, h):
                copy.wait_recv()

        @pl.when(jnp.logical_and(inner, h < VIA_KEYS))
        def _():
            carry(0, h)

        @pl.when(jnp.logical_and(jnp.logical_and(inner, has_link), h + LEAD < chunks))
        def _():
            start_link_keys(h + LEAD)

        for copy in key_copies(CHIP, to_chip, h):
            copy.wait_recv()

        @pl.when(has_link)
        def _():
            for copy in key_copies(LINK, to_link, h):
                copy.wait_recv()

        @pl.when(outer)
        def _():
            for copy in key_copies(FAR, to_chip, h):
                copy.start()

        def own_keys(sources):
            dk_own[:, at], dv_own[:, at] = pair_block(h, 0, sources, fresh=True)
            if ACROSS not in sources:
                dq_sum[:, ACROSS * tile :] = jnp.zeros((width, tile), F32)

        def chip_keys(sources):
            dk, dv = pair_block(h, CHIP, sources)
            dk_send[CHIP - 1, :, at] = dk.astype(LOW)
            dv_send[CHIP - 1, :, at] = dv.astype(LOW)

        def link_keys(sources):
            held[lax.rem(h, 2), 0], held[lax.rem(h, 2), 1] = pair_block(h, LINK, sources)

        either(jnp.logical_or(inner, middle), own_keys, ALL, PAIR)
        either(inner, chip_keys, ALL, PAIR)
        for copy in dkv_copies(CHIP, to_chip, h):
            copy.start()

        @pl.when(has_link)
        def _():
            either(middle, link_keys, ALL, LAST)

        @pl.when(jnp.logical_and(inner, has_link))
        def _():
            dk_send[LINK - 1, :, at] = held[lax.rem(h, 2), 0].astype(LOW)
            dv_send[LINK - 1, :, at] = held[lax.rem(h, 2), 1].astype(LOW)
            send_link_grads(h)

        @pl.when(outer)
        def _():
            for copy in key_copies(FAR, to_chip, h):
                copy.wait_recv()
            dk, dv = pair_block(h, FAR, LAST)
            dk_send[FAR - 1, :, at] = dk.astype(LOW)
            dv_send[FAR - 1, :, at] = dv.astype(LOW)
            for copy in dkv_copies(FAR, to_chip, h):
                copy.start()

        finish_queries(h)
        start_dq(h)

        @pl.when(jnp.logical_and(outer, h >= 1))
        def _():
            merge(h - 1)

    loop(0, chunks, compute)

    @pl.when(outer)
    def _():
        merge(chunks - 1)

    @pl.when(inner)
    def _():
        loop(0, VIA_GRADS, lambda c: carry(1, c))

    @pl.when(jnp.logical_not(has_link))
    def _():
        dk_recv[LINK - 1] = jnp.zeros((tile, full), LOW)
        dv_recv[LINK - 1] = jnp.zeros((tile, full), LOW)

    @pl.when(jnp.logical_not(has_across))
    def _():
        dq_recv[ACROSS - 1] = jnp.zeros((tile, full), LOW)

    def last_pass(c):
        at = cols(c)
        dq_copy(NEAR, c).wait_recv()

        @pl.when(has_across)
        def _():
            dq_copy(ACROSS, c).wait_recv()

        for copy in dkv_copies(CHIP, to_chip, c):
            copy.wait_recv()
        @pl.when(has_link)
        def _():
            for copy in dkv_copies(LINK, to_link, c):
                copy.wait_recv()
        for own, recv, out in ((dq_own, dq_recv, dq_out), (dk_own, dk_recv, dk_out), (dv_own, dv_recv, dv_out)):
            out[:, at] = (own[:, at] + recv[0, :, at].astype(F32) + recv[1, :, at].astype(F32)).astype(LOW)

    loop(0, chunks, last_pass)

    aux_copy(NEAR).wait_send()

    @pl.when(has_across)
    def _():
        aux_copy(ACROSS).wait_send()

    def drain(c):
        for copy in (*query_copies(NEAR, c), dq_copy(NEAR, c)):
            copy.wait_send()

        @pl.when(has_across)
        def _():
            for copy in (*query_copies(ACROSS, c), dq_copy(ACROSS, c)):
                copy.wait_send()

        for copy in (*key_copies(CHIP, to_chip, c), *dkv_copies(CHIP, to_chip, c)):
            copy.wait_send()
        @pl.when(has_link)
        def _():
            for copy in (*key_copies(LINK, to_link, c), *dkv_copies(LINK, to_link, c)):
                copy.wait_send()
        @pl.when(outer)
        def _():
            for copy in (*key_copies(FAR, to_chip, c), *dkv_copies(FAR, to_chip, c)):
                copy.wait_send()

    loop(0, chunks, drain)

    def drain_carried(kind):
        def run(c):
            for copy in onward_copies(kind, c):
                copy.wait_send()

        return run

    @pl.when(inner)
    def _():
        loop(0, VIA_KEYS, drain_carried(0))
        loop(0, VIA_GRADS, drain_carried(1))


def per_device(queries, keys, values, outputs, out_grads, log_sums, window_mask):
    shape = queries.shape
    tile, full = shape[2:]
    heads = log_sums.shape[2]
    width = full // heads
    chunks = heads
    flat = (tile, full)
    any_spec = pl.BlockSpec(memory_space=pl.ANY)
    vmem = pl.BlockSpec(memory_space=pltpu.VMEM)
    dma = pltpu.SemaphoreType.DMA
    grads = pl.pallas_call(
        kernel,
        out_shape=(jax.ShapeDtypeStruct(flat, LOW),) * 3,
        in_specs=[any_spec] * 5 + [vmem, pl.BlockSpec(memory_space=pltpu.SMEM)],
        out_specs=(vmem,) * 3,
        scratch_shapes=[
            *[pltpu.VMEM((3,) + flat, LOW)] * 2,
            *[pltpu.VMEM((4,) + flat, LOW)] * 2,
            pltpu.VMEM(flat, LOW),
            pltpu.VMEM((3, AUX_ROWS, tile), F32),
            pltpu.VMEM((width, 3 * tile), F32),
            pltpu.VMEM((2, 2, tile, width), F32),
            *[pltpu.VMEM(flat, F32)] * 3,
            pltpu.VMEM((2,) + flat, LOW), *[pltpu.VMEM((3,) + flat, LOW)] * 2,
            pltpu.VMEM((2,) + flat, LOW), *[pltpu.VMEM((3,) + flat, LOW)] * 2,
            pltpu.VMEM((2, 2, tile, max(VIA_KEYS, VIA_GRADS) * width), LOW),
            dma((5,)), dma((2, 2, chunks)), dma((2, 2, chunks)),
            dma((2, 2, chunks)), dma((2, 2, chunks)),
            dma((3, 2, chunks)), dma((3, 2, chunks)),
            dma((2,)), dma((2,)),
            dma((2, chunks)), dma((2, chunks)),
            dma((3, 2, chunks)), dma((3, 2, chunks)),
        ],
        compiler_params=pltpu.CompilerParams(
            collective_id=0, has_side_effects=True, vmem_limit_bytes=54 * 2**20
        ),
        name="tile_attention_backward",
    )(
        *[x.reshape(flat) for x in (queries, keys, values, outputs, out_grads)],
        log_sums.reshape(heads, 1, tile),
        window_mask.reshape(1, -1),
    )
    return tuple(g.reshape(shape) for g in grads)


def solution(mesh):
    tiles = P("tm", "space", None, None)
    return jax.shard_map(
        per_device,
        mesh=mesh,
        in_specs=(tiles,) * 6 + (P("tm", "space", None),),
        out_specs=(tiles,) * 3,
        check_vma=False,
    )
```

time: 127 us -> 121 us (0.953)
  Pallas kernels: 119 us -> 115 us
  local copies, waits for them, and re-layouts: 6.5 us -> 5.17 us
    pallas_call x1, Pallas kernels: 119 us -> 115 us  [per_device(): pl.pallas_call(kernel, out_shape=(jax.ShapeDtypeStruct(flat, LOW),) * 3,...]
    unnamed x8 -> x7, local copies, waits for them, and re-layouts: 6.5 us -> 5.17 us
where the time goes in v4:
time: 121 us
  Pallas kernels  115 us (95%)
  local copies, waits for them, and re-layouts  5.17 us (4%)
    pallas_call x1, Pallas kernels, per_device(): pl.pallas_call(kernel, out_shape=(jax.ShapeDtypeStruct(flat, LOW),) * 3,...  115 us
    unnamed x7, local copies, waits for them, and re-layouts  5.17 us

profile of v4, /device:TPU:5, one launch (start us, length us, event | category | flops | bytes accessed | tf_op | source)
XLA Modules:
  0.0 120.6 jit_solution(16633099290425801648)
XLA Ops:
  0.6 114.8 %tile_attention_backward.1 = (bf16[384,1536]{1,0:T(8,128)(2,1)}, bf16[384,1536]{1,0:T(8,128)(2,1)}, bf16[384,1536]{1,0:T(8,128)(2,1)}) custom-call(bf16[384,1536]{1,0:T(8,128)(2,1)} %bitcast.13, bf16[384,1536]{1,0:T(8,128)(2,1)} %bitcast.14, bf16[384,1536]{1,0:T(8,128)(2,1)} %bitcast.15, bf16[384,1536]{1,0:T(8,128)(2,1)} %bitcast.16, ...), custom_call_target="tpu_custom_call" | custom-call | tf_op jit(solution)/shard_map/tile_attention_backward/pallas_call | solution.py:465
  115.4 0.0 copy-start.1
  115.4 2.5 %copy.13 = bf16[1,1,384,1536]{3,2,1,0:T(8,128)(2,1)} copy(bf16[1,1,384,1536]{3,2,1,0:T(8,128)(2,1)} %bitcast.12) | data formatting | bytes 2359296
  117.9 0.0 copy-done.1
  117.9 0.0 copy-start
  117.9 1.0 copy.14
  118.9 0.7 copy-done
  119.6 1.0 copy.15
Async XLA Ops:
  115.4 2.5 %copy-start.1 = (bf16[384,1536]{1,0:T(8,128)(2,1)S(1)}, bf16[384,1536]{1,0:T(8,128)(2,1)}, u32[]{:S(2)}) copy-start(bf16[384,1536]{1,0:T(8,128)(2,1)} %get-tuple-element.7) | copy-start | bytes 3538948
  117.9 1.7 %copy-start = (bf16[384,1536]{1,0:T(8,128)(2,1)S(1)}, bf16[384,1536]{1,0:T(8,128)(2,1)}, u32[]{:S(2)}) copy-start(bf16[384,1536]{1,0:T(8,128)(2,1)} %get-tuple-element.8) | copy-start | bytes 3538948

commit v5 on v4

--- a/solution.py
+++ b/solution.py
@@ -19,7 +19,7 @@
 OWN, NEAR, ACROSS = 0, 1, 2
 CHIP, LINK, FAR = 1, 2, 3
 DELTA_ROW, PEN_ROW, AUX_ROWS = 12, 24, 40
-VIA_KEYS = 3
+VIA_KEYS = 2
 VIA_GRADS = 0
 LEAD = 3
 
@@ -31,9 +31,9 @@
 def kernel(
     q_in, k_in, v_in, o_in, g_in, lse_ref, mask_ref,
     dq_out, dk_out, dv_out,
-    qs, gs, ks, vs, outs, aux, dq_sum, held, dq_own, dk_own, dv_own,
+    qs, gs, ks, vs, aux, now, pens, across_sum, held, dq_own, dk_own, dv_own,
     dq_send, dk_send, dv_send, dq_recv, dk_recv, dv_recv, passing,
-    in_sem, pass_rs, pass_ss, q_ss, q_rs, kv_ss, kv_rs, aux_ss, aux_rs, dq_ss, dq_rs, dkv_ss, dkv_rs,
+    in_sem, out_sem, pass_rs, pass_ss, q_ss, q_rs, kv_ss, kv_rs, aux_ss, aux_rs, dq_ss, dq_rs, dkv_ss, dkv_rs,
 ):
     tile, full = q_in.shape
     heads = lse_ref.shape[0]
@@ -65,6 +65,7 @@
     def head_cols(h):
         return pl.ds(pl.multiple_of(h * width, width), width)
 
+    outs = dq_send.at[0]
     local = [
         pltpu.make_async_copy(src, dst, in_sem.at[i])
         for i, (src, dst) in enumerate(
@@ -223,57 +224,61 @@
     def _():
         aux_copy(ACROSS).wait_recv()
 
+    for slot in (0, CHIP, LINK, FAR):
+        for source, (query_frame, row_offset) in enumerate(query_frames):
+            offset = jnp.clip(key_frames[slot] - query_frame, -1, 1)
+            table = aux[source, PEN_ROW : PEN_ROW + 16, :]
+            chosen = lax.broadcasted_iota(jnp.int32, table.shape, 0) == 3 * (offset + 1) + row_offset + 1
+            line = jnp.sum(jnp.where(chosen, table, 0.0), 0, keepdims=True)
+            pens[slot : slot + 1, source * tile : (source + 1) * tile] = line
+
     def pick(table, index):
         chosen = lax.broadcasted_iota(jnp.int32, table.shape, 0) == index
         return jnp.sum(jnp.where(chosen, table, 0.0), 0, keepdims=True)
 
-    def pair_block(h, slot, sources, fresh=False):
+    def pair_block(h, slot, sources):
         at = head_cols(h)
         first, count = sources[0], len(sources)
+        span = slice(first * tile, (first + count) * tile)
         q = qs[first : first + count, :, at].reshape(count * tile, width)
         g = gs[first : first + count, :, at].reshape(count * tile, width)
         k, v = ks[slot, :, at], vs[slot, :, at]
-        lines, deltas = [], []
-        for source in sources:
-            query_frame, row_offset = query_frames[source]
-            table = aux[source]
-            pen = PEN_ROW + 3 * (key_frames[slot] - query_frame + 1) + row_offset + 1
-            lines.append(pick(table, h) + pick(table, pen))
-            deltas.append(pick(table, DELTA_ROW + h))
-        line, delta = jnp.concatenate(lines, 1), jnp.concatenate(deltas, 1)
+        line = now[0:1, span] + pens[slot : slot + 1, span]
         weights = jnp.exp2(dot(k, q, NT) * (scale * LOG2E) - line)
-        grad_score = (weights * (dot(v, g, NT) - delta)).astype(LOW)
-        span = slice(first * tile, (first + count) * tile)
-        more = dot(k, grad_score, TN)
-        dq_sum[:, span] = more if fresh else dq_sum[:, span] + more
-        return dot(grad_score, q, NN) * scale, dot(weights.astype(LOW), g, NN)
+        grad_score = (weights * (dot(v, g, NT) - now[1:2, span])).astype(LOW)
+        dk = dot(grad_score, q, NN) * scale
+        dv = dot(weights.astype(LOW), g, NN)
+        return dk, dv, dot(k, grad_score, TN)
 
     ALL, PAIR, LAST = (OWN, NEAR, ACROSS), (OWN, NEAR), (ACROSS,)
 
-    def either(condition, body, yes, no):
-        @pl.when(condition)
-        def _():
-            body(yes)
-
-        @pl.when(jnp.logical_not(condition))
-        def _():
-            body(no)
-
-    def finish_queries(h):
+    def finish_queries(h, source, total):
+        part = total.T * scale
+        if source == OWN:
+            dq_own[:, head_cols(h)] = part
+        else:
+            dq_send[source - 1, :, head_cols(h)] = part.astype(LOW)
+
+    def role(h, blocks, is_outer):
         at = head_cols(h)
-        for source in (OWN, NEAR, ACROSS):
-            part = dq_sum[:, source * tile : (source + 1) * tile].T * scale
-            if source == OWN:
-                dq_own[:, at] = part
+        totals = {}
+        for slot, sources in blocks:
+            dk, dv, more = pair_block(h, slot, sources)
+            for i, source in enumerate(sources):
+                piece = more[:, i * tile : (i + 1) * tile]
+                totals[source] = totals[source] + piece if source in totals else piece
+            if slot == 0:
+                dk_own[:, at], dv_own[:, at] = dk, dv
+            elif slot == LINK and is_outer:
+                held[lax.rem(h, 2), 0], held[lax.rem(h, 2), 1] = dk, dv
             else:
-                dq_send[source - 1, :, at] = part.astype(LOW)
-
-    def start_dq(c):
-        dq_copy(NEAR, c).start()
-
-        @pl.when(has_across)
-        def _():
-            dq_copy(ACROSS, c).start()
+                dk_send[slot - 1, :, at] = dk.astype(LOW)
+                dv_send[slot - 1, :, at] = dv.astype(LOW)
+        for source, total in totals.items():
+            if source == ACROSS and is_outer:
+                across_sum[...] = total
+            else:
+                finish_queries(h, source, total)
 
     def send_link_grads(c):
         relayed = jnp.logical_and(outer, c < VIA_GRADS)
@@ -328,46 +333,44 @@
             for copy in key_copies(FAR, to_chip, h):
                 copy.start()
 
-        def own_keys(sources):
-            dk_own[:, at], dv_own[:, at] = pair_block(h, 0, sources, fresh=True)
-            if ACROSS not in sources:
-                dq_sum[:, ACROSS * tile :] = jnp.zeros((width, tile), F32)
-
-        def chip_keys(sources):
-            dk, dv = pair_block(h, CHIP, sources)
-            dk_send[CHIP - 1, :, at] = dk.astype(LOW)
-            dv_send[CHIP - 1, :, at] = dv.astype(LOW)
-
-        def link_keys(sources):
-            held[lax.rem(h, 2), 0], held[lax.rem(h, 2), 1] = pair_block(h, LINK, sources)
-
-        either(jnp.logical_or(inner, middle), own_keys, ALL, PAIR)
-        either(inner, chip_keys, ALL, PAIR)
+        for source in (OWN, NEAR, ACROSS):
+            span = slice(source * tile, (source + 1) * tile)
+            table = aux[source]
+            now[0:1, span] = pick(table, h)
+            now[1:2, span] = pick(table, DELTA_ROW + h)
+
+        for here, blocks, is_outer in (
+            (jnp.logical_and(outer, middle), ((0, ALL), (CHIP, PAIR), (LINK, ALL)), True),
+            (jnp.logical_and(outer, jnp.logical_not(middle)), ((0, PAIR), (CHIP, PAIR), (LINK, LAST)), True),
+            (jnp.logical_and(inner, middle), ((0, ALL), (CHIP, ALL), (LINK, ALL)), False),
+            (jnp.logical_and(inner, jnp.logical_not(middle)), ((0, ALL), (CHIP, ALL)), False),
+        ):
+            @pl.when(here)
+            def _():
+                role(h, blocks, is_outer)
+
         for copy in dkv_copies(CHIP, to_chip, h):
             copy.start()
-
-        @pl.when(has_link)
-        def _():
-            either(middle, link_keys, ALL, LAST)
+        dq_copy(NEAR, h).start()
 
         @pl.when(jnp.logical_and(inner, has_link))
         def _():
-            dk_send[LINK - 1, :, at] = held[lax.rem(h, 2), 0].astype(LOW)
-            dv_send[LINK - 1, :, at] = held[lax.rem(h, 2), 1].astype(LOW)
             send_link_grads(h)
 
         @pl.when(outer)
         def _():
             for copy in key_copies(FAR, to_chip, h):
                 copy.wait_recv()
-            dk, dv = pair_block(h, FAR, LAST)
+            dk, dv, more = pair_block(h, FAR, LAST)
             dk_send[FAR - 1, :, at] = dk.astype(LOW)
             dv_send[FAR - 1, :, at] = dv.astype(LOW)
+            finish_queries(h, ACROSS, across_sum[...] + more)
             for copy in dkv_copies(FAR, to_chip, h):
                 copy.start()
 
-        finish_queries(h)
-        start_dq(h)
+        @pl.when(has_across)
+        def _():
+            dq_copy(ACROSS, h).start()
 
         @pl.when(jnp.logical_and(outer, h >= 1))
         def _():
@@ -391,6 +394,12 @@
     @pl.when(jnp.logical_not(has_across))
     def _():
         dq_recv[ACROSS - 1] = jnp.zeros((tile, full), LOW)
+
+    results = ((dq_own, dq_recv, qs.at[OWN]), (dk_own, dk_recv, ks.at[0]), (dv_own, dv_recv, vs.at[0]))
+
+    def out_copy(i, c):
+        out = (dq_out, dk_out, dv_out)[i]
+        return pltpu.make_async_copy(results[i][2].at[:, cols(c)], out.at[:, cols(c)], out_sem.at[i, c])
 
     def last_pass(c):
         at = cols(c)
@@ -406,8 +415,9 @@
         def _():
             for copy in dkv_copies(LINK, to_link, c):
                 copy.wait_recv()
-        for own, recv, out in ((dq_own, dq_recv, dq_out), (dk_own, dk_recv, dk_out), (dv_own, dv_recv, dv_out)):
-            out[:, at] = (own[:, at] + recv[0, :, at].astype(F32) + recv[1, :, at].astype(F32)).astype(LOW)
+        for i, (own, recv, stage) in enumerate(results):
+            stage[:, at] = (own[:, at] + recv[0, :, at].astype(F32) + recv[1, :, at].astype(F32)).astype(LOW)
+            out_copy(i, c).start()
 
     loop(0, chunks, last_pass)
 
@@ -418,6 +428,8 @@
         aux_copy(ACROSS).wait_send()
 
     def drain(c):
+        for i in range(3):
+            out_copy(i, c).wait()
         for copy in (*query_copies(NEAR, c), dq_copy(NEAR, c)):
             copy.wait_send()
 
@@ -465,20 +477,21 @@
     grads = pl.pallas_call(
         kernel,
         out_shape=(jax.ShapeDtypeStruct(flat, LOW),) * 3,
-        in_specs=[any_spec] * 5 + [vmem, pl.BlockSpec(memory_space=pltpu.SMEM)],
-        out_specs=(vmem,) * 3,
+        in_specs=[pl.BlockSpec(memory_space=pltpu.HBM)] * 5 + [vmem, pl.BlockSpec(memory_space=pltpu.SMEM)],
+        out_specs=(any_spec,) * 3,
         scratch_shapes=[
             *[pltpu.VMEM((3,) + flat, LOW)] * 2,
             *[pltpu.VMEM((4,) + flat, LOW)] * 2,
-            pltpu.VMEM(flat, LOW),
             pltpu.VMEM((3, AUX_ROWS, tile), F32),
-            pltpu.VMEM((width, 3 * tile), F32),
+            pltpu.VMEM((8, 3 * tile), F32),
+            pltpu.VMEM((8, 3 * tile), F32),
+            pltpu.VMEM((width, tile), F32),
             pltpu.VMEM((2, 2, tile, width), F32),
             *[pltpu.VMEM(flat, F32)] * 3,
             pltpu.VMEM((2,) + flat, LOW), *[pltpu.VMEM((3,) + flat, LOW)] * 2,
             pltpu.VMEM((2,) + flat, LOW), *[pltpu.VMEM((3,) + flat, LOW)] * 2,
             pltpu.VMEM((2, 2, tile, max(VIA_KEYS, VIA_GRADS) * width), LOW),
-            dma((5,)), dma((2, 2, chunks)), dma((2, 2, chunks)),
+            dma((5,)), dma((3, chunks)), dma((2, 2, chunks)), dma((2, 2, chunks)),
             dma((2, 2, chunks)), dma((2, 2, chunks)),
             dma((3, 2, chunks)), dma((3, 2, chunks)),
             dma((2,)), dma((2,)),
@@ -486,7 +499,7 @@
             dma((3, 2, chunks)), dma((3, 2, chunks)),
         ],
         compiler_params=pltpu.CompilerParams(
-            collective_id=0, has_side_effects=True, vmem_limit_bytes=54 * 2**20
+            collective_id=0, has_side_effects=True, vmem_limit_bytes=50 * 2**20
         ),
         name="tile_attention_backward",
     )(

time: 121 us -> 113 us (0.934)
  Pallas kernels: 115 us -> 107 us
    pallas_call x1, Pallas kernels: 115 us -> 107 us  [per_device(): pl.pallas_call(kernel, out_shape=(jax.ShapeDtypeStruct(flat, LOW),) * 3,...]
where the time goes in v5:
time: 113 us; the launch traced here: 112 us
  Pallas kernels  107 us (95%)
  local copies, waits for them, and re-layouts  4.41 us (4%)
    pallas_call x1, Pallas kernels, per_device(): pl.pallas_call(kernel, out_shape=(jax.ShapeDtypeStruct(flat, LOW),) * 3,...  107 us
    unnamed x7, local copies, waits for them, and re-layouts  4.41 us

profile of v5, /device:TPU:5, one launch (start us, length us, event | category | flops | bytes accessed | tf_op | source)
XLA Modules:
  0.0 112.4 jit_solution(12784990486775964889)
XLA Ops:
  0.6 0.0 copy-start
  0.6 0.7 copy-done
  1.4 0.0 copy-start.1
  1.4 0.7 copy-done.1
  2.0 107.3 %tile_attention_backward.1 = (bf16[384,1536]{1,0:T(8,128)(2,1)S(1)}, bf16[384,1536]{1,0:T(8,128)(2,1)S(1)}, bf16[384,1536]{1,0:T(8,128)(2,1)S(1)}) custom-call(bf16[384,1536]{1,0:T(8,128)(2,1)} %bitcast.15, bf16[384,1536]{1,0:T(8,128)(2,1)} %bitcast.16, bf16[384,1536]{1,0:T(8,128)(2,1)} %bitcast.17, bf16[384,1536]{1,0:T(8,128)(2,1)} %bitcast.18, ...), custom_call_target="tpu_custom_call" | custom-call | tf_op jit(solution)/shard_map/tile_attention_backward/pallas_call | solution.py:477
  109.3 1.0 copy.13
  110.3 1.0 copy.14
  111.3 1.0 copy.15
Async XLA Ops:
  0.6 0.7 copy-start
  1.4 0.7 copy-start.1

commit v6 on v5

--- a/solution.py
+++ b/solution.py
@@ -19,8 +19,7 @@
 OWN, NEAR, ACROSS = 0, 1, 2
 CHIP, LINK, FAR = 1, 2, 3
 DELTA_ROW, PEN_ROW, AUX_ROWS = 12, 24, 40
-VIA_KEYS = 2
-VIA_GRADS = 0
+VIA_FIRST, VIA_LAST = 8, 11
 LEAD = 3
 
 
@@ -123,24 +122,25 @@
             remote(dv_send.at[slot - 1, :, cols(c)], dv_recv.at[slot - 1, :, cols(c)], dkv_ss.at[slot - 1, 1, c], dkv_rs.at[slot - 1, 1, c], target),
         )
 
-    def via_copies(kind, c):
-        sources, ss = (((k_in, v_in), kv_ss), ((dk_send.at[LINK - 1], dv_send.at[LINK - 1]), dkv_ss))[kind]
+    def is_via(c):
+        return jnp.logical_and(c >= VIA_FIRST, c < VIA_LAST)
+
+    def via_copies(c):
         return [
-            remote(src.at[:, cols(c)], passing.at[kind, i, :, cols(c)], ss.at[LINK - 1, i, c], pass_rs.at[kind, i, c], to_near)
-            for i, src in enumerate(sources)
+            remote(src.at[:, cols(c)], passing.at[i, :, cols(c - VIA_FIRST)], kv_ss.at[LINK - 1, i, c], pass_rs.at[i, c], to_near)
+            for i, src in enumerate((k_in, v_in))
         ]
 
-    def onward_copies(kind, c):
-        targets, rs = (((ks.at[LINK], vs.at[LINK]), kv_rs), ((dk_recv.at[LINK - 1], dv_recv.at[LINK - 1]), dkv_rs))[kind]
+    def onward_copies(c):
         return [
-            remote(passing.at[kind, i, :, cols(c)], dst.at[:, cols(c)], pass_ss.at[kind, i, c], rs.at[LINK - 1, i, c], to_cross)
-            for i, dst in enumerate(targets)
+            remote(passing.at[i, :, cols(c - VIA_FIRST)], dst.at[LINK, :, cols(c)], pass_ss.at[i, c], kv_rs.at[LINK - 1, i, c], to_cross)
+            for i, dst in enumerate((ks, vs))
         ]
 
-    def carry(kind, c):
-        for copy in via_copies(kind, c):
+    def carry(c):
+        for copy in via_copies(c):
             copy.wait_recv()
-        for copy in onward_copies(kind, c):
+        for copy in onward_copies(c):
             copy.start()
 
     def loop(first, last, body):
@@ -151,9 +151,9 @@
         lax.fori_loop(first, last, run, 0)
 
     def start_queries(c):
-        @pl.when(jnp.logical_and(outer, c < VIA_KEYS))
-        def _():
-            for copy in via_copies(0, c):
+        @pl.when(jnp.logical_and(outer, is_via(c)))
+        def _():
+            for copy in via_copies(c):
                 copy.start()
         for copy in query_copies(NEAR, c):
             copy.start()
@@ -180,7 +180,8 @@
 
     @pl.when(outer)
     def _():
-        loop(VIA_KEYS, chunks, start_link_keys)
+        loop(0, VIA_FIRST, start_link_keys)
+        loop(VIA_LAST, chunks, start_link_keys)
 
     local[0].wait()
     local[1].wait()
@@ -281,17 +282,8 @@
                 finish_queries(h, source, total)
 
     def send_link_grads(c):
-        relayed = jnp.logical_and(outer, c < VIA_GRADS)
-
-        @pl.when(relayed)
-        def _():
-            for copy in via_copies(1, c):
-                copy.start()
-
-        @pl.when(jnp.logical_not(relayed))
-        def _():
-            for copy in dkv_copies(LINK, to_link, c):
-                copy.start()
+        for copy in dkv_copies(LINK, to_link, c):
+            copy.start()
 
     def merge(c):
         at = head_cols(c)
@@ -312,9 +304,9 @@
             for copy in query_copies(ACROSS, h):
                 copy.wait_recv()
 
-        @pl.when(jnp.logical_and(inner, h < VIA_KEYS))
-        def _():
-            carry(0, h)
+        @pl.when(jnp.logical_and(inner, is_via(h)))
+        def _():
+            carry(h)
 
         @pl.when(jnp.logical_and(jnp.logical_and(inner, has_link), h + LEAD < chunks))
         def _():
@@ -382,10 +374,6 @@
     def _():
         merge(chunks - 1)
 
-    @pl.when(inner)
-    def _():
-        loop(0, VIA_GRADS, lambda c: carry(1, c))
-
     @pl.when(jnp.logical_not(has_link))
     def _():
         dk_recv[LINK - 1] = jnp.zeros((tile, full), LOW)
@@ -451,17 +439,13 @@
 
     loop(0, chunks, drain)
 
-    def drain_carried(kind):
-        def run(c):
-            for copy in onward_copies(kind, c):
-                copy.wait_send()
-
-        return run
+    def drain_carried(c):
+        for copy in onward_copies(c):
+            copy.wait_send()
 
     @pl.when(inner)
     def _():
-        loop(0, VIA_KEYS, drain_carried(0))
-        loop(0, VIA_GRADS, drain_carried(1))
+        loop(VIA_FIRST, VIA_LAST, drain_carried)
 
 
 def per_device(queries, keys, values, outputs, out_grads, log_sums, window_mask):
@@ -490,8 +474,8 @@
             *[pltpu.VMEM(flat, F32)] * 3,
             pltpu.VMEM((2,) + flat, LOW), *[pltpu.VMEM((3,) + flat, LOW)] * 2,
             pltpu.VMEM((2,) + flat, LOW), *[pltpu.VMEM((3,) + flat, LOW)] * 2,
-            pltpu.VMEM((2, 2, tile, max(VIA_KEYS, VIA_GRADS) * width), LOW),
-            dma((5,)), dma((3, chunks)), dma((2, 2, chunks)), dma((2, 2, chunks)),
+            pltpu.VMEM((2, tile, (VIA_LAST - VIA_FIRST) * width), LOW),
+            dma((5,)), dma((3, chunks)), dma((2, chunks)), dma((2, chunks)),
             dma((2, 2, chunks)), dma((2, 2, chunks)),
             dma((3, 2, chunks)), dma((3, 2, chunks)),
             dma((2,)), dma((2,)),

time: 113 us -> 109 us (0.965)
  Pallas kernels: 107 us -> 103 us
    pallas_call x1, Pallas kernels: 107 us -> 103 us  [per_device(): pl.pallas_call(kernel, out_shape=(jax.ShapeDtypeStruct(flat, LOW),) * 3,...]
where the time goes in v6:
time: 109 us; the launch traced here: 108 us
  Pallas kernels  103 us (94%)
  local copies, waits for them, and re-layouts  4.41 us (4%)
    pallas_call x1, Pallas kernels, per_device(): pl.pallas_call(kernel, out_shape=(jax.ShapeDtypeStruct(flat, LOW),) * 3,...  103 us
    unnamed x7, local copies, waits for them, and re-layouts  4.41 us

profile of v6, /device:TPU:5, one launch (start us, length us, event | category | flops | bytes accessed | tf_op | source)
XLA Modules:
  0.0 107.7 jit_solution(14003586271937841907)
XLA Ops:
  0.6 0.0 copy-start
  0.6 0.7 copy-done
  1.4 0.0 copy-start.1
  1.4 0.7 copy-done.1
  2.0 102.6 %tile_attention_backward.1 = (bf16[384,1536]{1,0:T(8,128)(2,1)S(1)}, bf16[384,1536]{1,0:T(8,128)(2,1)S(1)}, bf16[384,1536]{1,0:T(8,128)(2,1)S(1)}) custom-call(bf16[384,1536]{1,0:T(8,128)(2,1)} %bitcast.15, bf16[384,1536]{1,0:T(8,128)(2,1)} %bitcast.16, bf16[384,1536]{1,0:T(8,128)(2,1)} %bitcast.17, bf16[384,1536]{1,0:T(8,128)(2,1)} %bitcast.18, ...), custom_call_target="tpu_custom_call" | custom-call | tf_op jit(solution)/shard_map/tile_attention_backward/pallas_call | solution.py:461
  104.6 1.0 copy.13
  105.7 1.0 copy.14
  106.7 1.0 copy.15
Async XLA Ops:
  0.6 0.7 copy-start
  1.4 0.7 copy-start.1

commit v7 on v6

--- a/solution.py
+++ b/solution.py
@@ -446,6 +446,15 @@
     @pl.when(inner)
     def _():
         loop(VIA_FIRST, VIA_LAST, drain_carried)
+
+
+def store_kernel(*refs):
+    sources, targets, sem = refs[:3], refs[3:6], refs[6]
+    copies = [pltpu.make_async_copy(a, b, sem.at[i]) for i, (a, b) in enumerate(zip(sources, targets))]
+    for copy in copies:
+        copy.start()
+    for copy in copies:
+        copy.wait()
 
 
 def per_device(queries, keys, values, outputs, out_grads, log_sums, window_mask):
@@ -491,7 +500,16 @@
         log_sums.reshape(heads, 1, tile),
         window_mask.reshape(1, -1),
     )
-    return tuple(g.reshape(shape) for g in grads)
+    stored = pl.pallas_call(
+        store_kernel,
+        out_shape=(jax.ShapeDtypeStruct(flat, LOW),) * 3,
+        in_specs=[vmem] * 3,
+        out_specs=(pl.BlockSpec(memory_space=pltpu.HBM),) * 3,
+        scratch_shapes=[dma((3,))],
+        compiler_params=pltpu.CompilerParams(vmem_limit_bytes=8 * 2**20),
+        name="store_gradients",
+    )(*grads)
+    return tuple(g.reshape(shape) for g in stored)
 
 
 def solution(mesh):

time: 109 us -> 108 us (level)
  local copies, waits for them, and re-layouts: 4.41 us -> 1.37 us
    unnamed x7 -> x4, local copies, waits for them, and re-layouts: 4.41 us -> 1.37 us
    pallas_call x0 -> x1, Pallas kernels: none -> 1.82 us  [per_device(): pl.pallas_call(store_kernel, out_shape=(jax.ShapeDtypeStruct(flat, LOW),)...]
where the time goes in v7:
time: 108 us; the launch traced here: 106 us
  Pallas kernels  104 us (96%)
  local copies, waits for them, and re-layouts  1.37 us (1%)
    pallas_call x1, Pallas kernels, per_device(): pl.pallas_call(kernel, out_shape=(jax.ShapeDtypeStruct(flat, LOW),) * 3,...  103 us

profile of v7, /device:TPU:5, one launch (start us, length us, event | category | flops | bytes accessed | tf_op | source)
XLA Modules:
  0.0 106.5 jit_solution(14686078815671368166)
XLA Ops:
  0.6 0.0 copy-start
  0.6 0.7 copy-done
  1.4 0.0 copy-start.1
  1.4 0.7 copy-done.1
  2.0 102.6 %tile_attention_backward.1 = (bf16[384,1536]{1,0:T(8,128)(2,1)S(1)}, bf16[384,1536]{1,0:T(8,128)(2,1)S(1)}, bf16[384,1536]{1,0:T(8,128)(2,1)S(1)}) custom-call(bf16[384,1536]{1,0:T(8,128)(2,1)} %bitcast.12, bf16[384,1536]{1,0:T(8,128)(2,1)} %bitcast.13, bf16[384,1536]{1,0:T(8,128)(2,1)} %bitcast.14, bf16[384,1536]{1,0:T(8,128)(2,1)} %bitcast.15, ...), custom_call_target="tpu_custom_call" | custom-call | tf_op jit(solution)/shard_map/tile_attention_backward/pallas_call | solution.py:470
  104.6 1.8 %store_gradients.1 = (bf16[384,1536]{1,0:T(8,128)(2,1)}, bf16[384,1536]{1,0:T(8,128)(2,1)}, bf16[384,1536]{1,0:T(8,128)(2,1)}) custom-call(bf16[384,1536]{1,0:T(8,128)(2,1)S(1)} %get-tuple-element.9.refs_0_, bf16[384,1536]{1,0:T(8,128)(2,1)S(1)} %get-tuple-element.10.refs_1_, bf16[384,1536]{1,0:T(8,128)(2,1)S(1)} %get-tuple-element.11.refs_2_), custom_call_target="tpu_custom_call" | custom-call | tf_op jit(solution)/shard_map/store_gradients/pallas_call | solution.py:503
Async XLA Ops:
  0.6 0.7 copy-start
  1.4 0.7 copy-start.1

commit v8 on v7

--- a/solution.py
+++ b/solution.py
@@ -28,9 +28,9 @@
 
 
 def kernel(
-    q_in, k_in, v_in, o_in, g_in, lse_ref, mask_ref,
+    q_in, k_in, v_in, o_in, g_in, lse_in, mask_in,
     dq_out, dk_out, dv_out,
-    qs, gs, ks, vs, aux, now, pens, across_sum, held, dq_own, dk_own, dv_own,
+    lse_ref, mask_ref, qs, gs, ks, vs, aux, now, pens, across_sum, held, dq_own, dk_own, dv_own,
     dq_send, dk_send, dv_send, dq_recv, dk_recv, dv_recv, passing,
     in_sem, out_sem, pass_rs, pass_ss, q_ss, q_rs, kv_ss, kv_rs, aux_ss, aux_rs, dq_ss, dq_rs, dkv_ss, dkv_rs,
 ):
@@ -68,11 +68,12 @@
     local = [
         pltpu.make_async_copy(src, dst, in_sem.at[i])
         for i, (src, dst) in enumerate(
-            ((o_in, outs), (g_in, gs.at[OWN]), (q_in, qs.at[OWN]), (k_in, ks.at[0]), (v_in, vs.at[0]))
+            (
+                (o_in, outs), (g_in, gs.at[OWN]), (lse_in, lse_ref), (mask_in, mask_ref),
+                (q_in, qs.at[OWN]), (k_in, ks.at[0]), (v_in, vs.at[0]),
+            )
         )
     ]
-    for copy in local:
-        copy.start()
 
     barrier = pltpu.get_barrier_semaphore()
     pl.semaphore_signal(barrier, inc=1, device_id=to_chip, device_id_type=MESH)
@@ -82,6 +83,8 @@
         def _():
             pl.semaphore_signal(barrier, inc=1, device_id=dst, device_id_type=MESH)
     pl.semaphore_signal(barrier, inc=1, device_id=to_cross, device_id_type=MESH)
+    for copy in local:
+        copy.start()
     peers = 3 + has_across.astype(jnp.int32) + has_link.astype(jnp.int32)
     pl.semaphore_wait(barrier, peers)
 
@@ -183,8 +186,8 @@
         loop(0, VIA_FIRST, start_link_keys)
         loop(VIA_LAST, chunks, start_link_keys)
 
-    local[0].wait()
-    local[1].wait()
+    for copy in local[:4]:
+        copy.wait()
     aux[OWN] = jnp.zeros((AUX_ROWS, tile), F32)
     for h in range(heads):
         aux[OWN, h : h + 1, :] = lse_ref[h] * LOG2E
@@ -217,7 +220,7 @@
         gs[ACROSS] = jnp.zeros((tile, full), LOW)
         aux[ACROSS] = jnp.zeros((AUX_ROWS, tile), F32)
 
-    for copy in local[2:]:
+    for copy in local[4:]:
         copy.wait()
     aux_copy(NEAR).wait_recv()
 
@@ -470,9 +473,11 @@
     grads = pl.pallas_call(
         kernel,
         out_shape=(jax.ShapeDtypeStruct(flat, LOW),) * 3,
-        in_specs=[pl.BlockSpec(memory_space=pltpu.HBM)] * 5 + [vmem, pl.BlockSpec(memory_space=pltpu.SMEM)],
+        in_specs=[pl.BlockSpec(memory_space=pltpu.HBM)] * 7,
         out_specs=(any_spec,) * 3,
         scratch_shapes=[
+            pltpu.VMEM((heads, 1, tile), F32),
+            pltpu.SMEM((1, 9), jnp.int32),
             *[pltpu.VMEM((3,) + flat, LOW)] * 2,
             *[pltpu.VMEM((4,) + flat, LOW)] * 2,
             pltpu.VMEM((3, AUX_ROWS, tile), F32),
@@ -484,7 +489,7 @@
             pltpu.VMEM((2,) + flat, LOW), *[pltpu.VMEM((3,) + flat, LOW)] * 2,
             pltpu.VMEM((2,) + flat, LOW), *[pltpu.VMEM((3,) + flat, LOW)] * 2,
             pltpu.VMEM((2, tile, (VIA_LAST - VIA_FIRST) * width), LOW),
-            dma((5,)), dma((3, chunks)), dma((2, chunks)), dma((2, chunks)),
+            dma((7,)), dma((3, chunks)), dma((2, chunks)), dma((2, chunks)),
             dma((2, 2, chunks)), dma((2, 2, chunks)),
             dma((3, 2, chunks)), dma((3, 2, chunks)),
             dma((2,)), dma((2,)),

time: 108 us -> 107 us (level)
  no operation moved by 1% of the time
where the time goes in v8:
time: 107 us; the launch traced here: 106 us
  Pallas kernels  104 us (97%)
  local copies, waits for them, and re-layouts  1.37 us (1%)
    pallas_call x1, Pallas kernels, per_device(): pl.pallas_call(kernel, out_shape=(jax.ShapeDtypeStruct(flat, LOW),) * 3,...  102 us

profile of v8, /device:TPU:5, one launch (start us, length us, event | category | flops | bytes accessed | tf_op | source)
XLA Modules:
  0.0 105.9 jit_solution(11961928326824486243)
XLA Ops:
  0.6 0.0 copy-start
  0.6 0.7 copy-done
  1.4 0.0 copy-start.1
  1.4 0.7 copy-done.1
  2.0 102.1 %tile_attention_backward.1 = (bf16[384,1536]{1,0:T(8,128)(2,1)S(1)}, bf16[384,1536]{1,0:T(8,128)(2,1)S(1)}, bf16[384,1536]{1,0:T(8,128)(2,1)S(1)}) custom-call(bf16[384,1536]{1,0:T(8,128)(2,1)} %bitcast.12, bf16[384,1536]{1,0:T(8,128)(2,1)} %bitcast.13, bf16[384,1536]{1,0:T(8,128)(2,1)} %bitcast.14, bf16[384,1536]{1,0:T(8,128)(2,1)} %bitcast.15, ...), custom_call_target="tpu_custom_call" | custom-call | tf_op jit(solution)/shard_map/tile_attention_backward/pallas_call | solution.py:473
  104.1 1.8 %store_gradients.1 = (bf16[384,1536]{1,0:T(8,128)(2,1)}, bf16[384,1536]{1,0:T(8,128)(2,1)}, bf16[384,1536]{1,0:T(8,128)(2,1)}) custom-call(bf16[384,1536]{1,0:T(8,128)(2,1)S(1)} %get-tuple-element.9.refs_0_, bf16[384,1536]{1,0:T(8,128)(2,1)S(1)} %get-tuple-element.10.refs_1_, bf16[384,1536]{1,0:T(8,128)(2,1)S(1)} %get-tuple-element.11.refs_2_), custom_call_target="tpu_custom_call" | custom-call | tf_op jit(solution)/shard_map/store_gradients/pallas_call | solution.py:508
Async XLA Ops:
  0.6 0.7 copy-start
  1.4 0.7 copy-start.1
